TPU v7x, 512 devices: a whole 4x8x8 slice. The times are simulated.
512 devices in a mesh: chan: 64 (over x, y, core), src: 8 (over z).
Axes of the slice: x: 4, y: 8, z: 8, core: 2. Of those that a mesh axis runs over, the one named last changes fastest.
Arguments:
- strain: bfloat16 [4096, 65536], P('src', 'chan'), may hold values from -6 to 6
- seg_start: int32 [3], replicated, may hold values from 0 to 8704
- src_chan: int32 [256], replicated, may hold values from 0 to 4095
Outputs:
- correlation: bfloat16 [256, 8, 512, 512], P('src', None, 'chan')
All inputs are finite; a program needn't handle non-finite values.
Results may differ from a plain program's by a relative error of at most 0.0083.
Values may be sent and summed in bfloat16 or wider, within the bound.
A program may use at most 64 MiB of HBM per device.

v0:
```python
import math

import jax
import jax.numpy as jnp
import numpy as np
from jax import lax
from jax.sharding import PartitionSpec as P

DEC = 4
SEG = 7680
NSEG = 3
BIN_LOW = 61
NBIN = 384
NLAG = 512


def decimation_tables():
    length = 4 * DEC
    offsets = np.arange(length)
    centred = (offsets - (length - 1) / 2.0) / DEC
    coeffs = (
        np.sin(np.pi * centred)
        / (np.pi * centred)
        * (0.54 - 0.46 * np.cos(2.0 * np.pi * (offsets + 0.5) / length))
    )
    coeffs = coeffs / coeffs.sum()
    sample_pos = np.arange(128)[:, None]
    output_pos = np.arange(128 // DEC)[None, :]
    tables = []
    for carried in (0, 128):
        tap_pos = sample_pos + carried - DEC * output_pos
        inside = (tap_pos >= 0) & (tap_pos < length)
        values = np.where(inside, coeffs[np.clip(tap_pos, 0, length - 1)], 0.0)
        tables.append(jnp.asarray(values, jnp.float32).astype(jnp.bfloat16))
    return (tables[0], tables[1])


def decimate(series, following, first_tab, second_tab):
    row_count, length = series.shape
    blocks = series.reshape(row_count, length // 128, 128)
    shifted = jnp.concatenate([blocks[:, 1:], following[:, None, :]], axis=1)
    summed = jnp.dot(blocks.reshape(-1, 128), first_tab, preferred_element_type=jnp.float32)
    summed = summed + jnp.dot(
        shifted.reshape(-1, 128), second_tab, preferred_element_type=jnp.float32
    )
    return summed.astype(jnp.bfloat16).reshape(row_count, length // DEC)


def whiten(spectrum):
    real_part = spectrum[..., :NBIN]
    imag_part = spectrum[..., NBIN:]
    energy = real_part * real_part + imag_part * imag_part
    offsets = np.arange(NBIN)
    band_mask = jnp.asarray((np.abs(offsets[:, None] - offsets[None, :]) <= 32).astype(np.float32))
    smooth = jnp.matmul(energy, band_mask, precision=lax.Precision.HIGHEST) / 65.0
    inverse = lax.rsqrt(smooth + 1e-05)
    return jnp.concatenate([real_part * inverse, imag_part * inverse], axis=-1).astype(jnp.bfloat16)


def lag_table():
    bin_ids = BIN_LOW + np.arange(NBIN)
    delays = np.arange(NLAG) - NLAG // 2
    angles = 2.0 * np.pi * np.mod(np.outer(bin_ids, delays), SEG) / SEG
    basis = np.concatenate([np.cos(angles), -np.sin(angles)], axis=0) / np.sqrt(NBIN)
    return jnp.asarray(basis, jnp.float32).astype(jnp.bfloat16)


def band_spectrum(segments):
    row_count = segments.shape[0]
    block_count = SEG // 512
    bin_ids = BIN_LOW + np.arange(NBIN)
    inner = 2.0 * np.pi * np.mod(np.outer(np.arange(512), bin_ids), SEG) / SEG
    table = jnp.asarray(np.concatenate([np.cos(inner), -np.sin(inner)], axis=1), jnp.float32)
    table_high = table.astype(jnp.bfloat16)
    table_low = (table - table_high.astype(jnp.float32)).astype(jnp.bfloat16)
    outer = 2.0 * np.pi * np.mod(np.outer(512 * np.arange(block_count), bin_ids), SEG) / SEG
    phase_cos = jnp.asarray(np.cos(outer), jnp.float32)
    phase_sin = jnp.asarray(np.sin(outer), jnp.float32)
    flat = segments.reshape(row_count * block_count, 512)
    partial_value = jnp.dot(flat, table_high, preferred_element_type=jnp.float32)
    partial_value = partial_value + jnp.dot(flat, table_low, preferred_element_type=jnp.float32)
    partial_value = partial_value.reshape(row_count, block_count, 2 * NBIN)
    part_re = partial_value[..., :NBIN]
    part_im = partial_value[..., NBIN:]
    total_re = jnp.sum(part_re * phase_cos + part_im * phase_sin, axis=1)
    total_im = jnp.sum(part_im * phase_cos - part_re * phase_sin, axis=1)
    return jnp.concatenate([total_re, total_im], axis=1) / math.sqrt(SEG)


def on_device(strain, seg_start, src_chan):
    first_tab, second_tab = decimation_tables()
    chan_count = lax.axis_size("chan")
    group_count = lax.axis_size("src")
    local_rows = strain.shape[0]
    per_device = local_rows // chan_count
    series = lax.all_to_all(strain, "chan", split_axis=0, concat_axis=1, tiled=True)
    padding = jnp.zeros((per_device, 128), jnp.bfloat16)
    decimated = decimate(series, padding, first_tab, second_tab)
    pieces = [
        lax.dynamic_slice_in_dim(decimated, seg_start[number], SEG, 1) for number in range(NSEG)
    ]
    segments = jnp.stack(pieces, axis=1).reshape(per_device * NSEG, SEG)
    spectra = whiten(band_spectrum(segments)).reshape(per_device, NSEG, 2 * NBIN)
    receivers = lax.all_gather(spectra, "src", axis=0, tiled=True)
    own_channels = (
        lax.axis_index("src") * local_rows
        + lax.axis_index("chan") * per_device
        + lax.iota(jnp.int32, per_device)
    )
    selector = (src_chan[:, None] == own_channels[None, :]).astype(jnp.bfloat16)
    picked = jnp.dot(
        selector, spectra.reshape(per_device, NSEG * 2 * NBIN), preferred_element_type=jnp.float32
    )
    summed_all = lax.psum(picked, "chan")
    grouped = lax.psum_scatter(
        summed_all.astype(jnp.bfloat16), "src", scatter_dimension=0, tiled=True
    )
    sources = grouped.reshape(-1, NSEG, 2 * NBIN)
    source_re = sources[..., :NBIN]
    source_im = sources[..., NBIN:]
    recv_re = receivers[..., :NBIN]
    recv_im = receivers[..., NBIN:]
    cross_re = jnp.einsum("ksf,rsf->krf", source_re, recv_re, preferred_element_type=jnp.float32)
    cross_re = (
        cross_re
        + jnp.einsum("ksf,rsf->krf", source_im, recv_im, preferred_element_type=jnp.float32)
    ) / NSEG
    cross_im = jnp.einsum("ksf,rsf->krf", source_re, recv_im, preferred_element_type=jnp.float32)
    cross_im = (
        cross_im
        - jnp.einsum("ksf,rsf->krf", source_im, recv_re, preferred_element_type=jnp.float32)
    ) / NSEG
    merged = jnp.concatenate([cross_re, cross_im], axis=-1).astype(jnp.bfloat16)
    lagged = jnp.dot(merged.reshape(-1, 2 * NBIN), lag_table(), preferred_element_type=jnp.float32)
    return lagged.astype(jnp.bfloat16).reshape(sources.shape[0], group_count, per_device, NLAG)


def solution(mesh):
    return jax.shard_map(
        on_device,
        mesh=mesh,
        in_specs=(P("src", "chan"), P(), P()),
        out_specs=P("src", None, "chan", None),
        check_vma=False,
    )
```

profile of v0, /device:TPU:1, one launch (start us, length us, event | category | flops | bytes accessed | tf_op | source)
XLA Modules:
  0.0 395.9 jit_solution(6811412884966001803)
XLA Ops:
  6.5 11.6 %all-to-all-start = ((bf16[64,8,1024]{2,1,0:T(8,128)(2,1)}), bf16[64,8,1024]{2,1,0:T(8,128)(2,1)S(1)}, u32[]{:S(2)}, u32[]{:S(2)}) async-start(bf16[64,8,1024]{2,1,0:T(8,128)(2,1)} %bitcast.47), calls=%async_computation | async-start | bytes 2097152 | tf_op jit(solution)/shard_map/all_to_all | solution.py:96
  18.2 1.4 fusion.14
  25.1 21.5 %all-to-all-done = bf16[64,8,1024]{2,1,0:T(8,128)(2,1)S(1)} async-done(((bf16[64,8,1024]{2,1,0:T(8,128)(2,1)}), bf16[64,8,1024]{2,1,0:T(8,128)(2,1)S(1)}, u32[]{:S(2)}, u32[]{:S(2)}) %all-to-all-start) | async-done | bytes 1048608 | tf_op jit(solution)/shard_map/all_to_all | solution.py:96
  46.7 0.6 copy.32
  47.3 0.5 reshape.42
  47.8 0.5 reshape_reshape.7
  48.6 0.5 convolution_bitcast_fusion
  49.2 0.5 fusion
  49.6 0.5 copy.34
  50.2 1.1 reshape.44
  53.7 0.5 copy-done.5
  54.7 0.5 fusion.5
  55.2 266.3 %all-reduce.2 = bf16[256,2304]{1,0:T(8,128)(2,1)} all-reduce(f32[256,2304]{1,0:T(8,128)S(1)} %fusion.5), channel_id=1, replica_groups=mesh['chan'=64,'src'=8] {'chan'}, use_global_device_ids=true, to_apply=%region_2.0 | all-reduce | flops 589824 | bytes 3538944 | tf_op jit(solution)/shard_map/psum | solution.py:114
  321.5 25.5 %all_gather.3 = bf16[64,3,768]{2,0,1:T(8,128)(2,1)S(1)} all-gather(bf16[8,3,768]{2,0,1:T(8,128)(2,1)S(1)} %pad_maximum_fusion.1), channel_id=1, replica_groups=mesh['chan'=64,'src'=8] {'src'}, dimensions={0}, use_global_device_ids=true | all-gather | bytes 331776 | tf_op jit(solution)/shard_map/all_gather | solution.py:104
  347.6 15.0 %reduce-scatter.2.cloned.1.call-done = bf16[32,2304]{1,0:T(8,128)(2,1)} async-done(((bf16[256,2304]{1,0:T(8,128)(2,1)}), bf16[32,2304]{1,0:T(8,128)(2,1)}) %reduce-scatter.2.cloned.1.call-update) | async-done | bytes 147472 | tf_op jit(solution)/shard_map/reduce_scatter | solution.py:115
  362.7 1.0 reshape.46
  364.3 1.0 fusion.18
  365.3 3.3 fusion.16
  368.6 2.5 fusion.2
  371.1 4.1 %copy.43 = bf16[32,64,384]{2,1,0:T(8,128)(2,1)} copy(bf16[32,64,384]{1,0,2:T(8,128)(2,1)S(1)} %fusion.2) | data formatting | bytes 3145728 | tf_op jit(solution)/shard_map/div | solution.py:129
  375.2 4.3 %fusion.1 = bf16[32,64,384]{1,0,2:T(8,128)(2,1)S(1)} fusion(f32[384,64,32]{1,2,0:T(8,128)} %fusion.16, bf16[64,3,384]{0,1,2:T(4,128)(2,1)} %copy-done.1, bf16[32,3,384]{0,1,2:T(4,128)(2,1)S(1)} %copy.47), kind=kOutput, calls=%fused_computation.6 | convolution fusion | flops 7077888 | bytes 4939776 | tf_op jit(solution)/shard_map/ksf,rsf->krf/dot_general | solution.py:126
  379.5 4.0 %copy.42 = bf16[32,64,384]{2,1,0:T(8,128)(2,1)} copy(bf16[32,64,384]{1,0,2:T(8,128)(2,1)S(1)} %fusion.1) | data formatting | bytes 3145728 | tf_op jit(solution)/shard_map/div | solution.py:124
  383.5 2.8 fusion.17
  386.3 2.7 add_convert_fusion
  (53 shorter events, 4.4 us)
Async XLA Ops:
  6.5 40.1 %all-to-all-start = ((bf16[64,8,1024]{2,1,0:T(8,128)(2,1)}), bf16[64,8,1024]{2,1,0:T(8,128)(2,1)S(1)}, u32[]{:S(2)}, u32[]{:S(2)}) async-start(bf16[64,8,1024]{2,1,0:T(8,128)(2,1)} %bitcast.47), calls=%async_computation | async-start | bytes 2097152 | tf_op jit(solution)/shard_map/all_to_all | solution.py:96
  18.2 344.5 %reduce-scatter.2.cloned.1.call-start = ((), (), s32[]{:S(2)}) async-start(), calls=%async_computation.2 | async-start | bytes 1327104 | tf_op jit(solution)/shard_map/reduce_scatter | solution.py:115
  47.3 1.3 copy-start.9
  48.3 0.9 copy-start.8
  49.6 2.5 copy-start.3
  50.1 2.5 copy-start.4
  52.6 0.7 copy-start.10
  52.6 0.7 copy-start.11
  52.6 2.0 copy-start.12
  53.1 1.1 copy-start.5
  347.4 17.9 %copy-start.1 = (bf16[64,3,384]{0,1,2:T(4,128)(2,1)}, bf16[64,3,384]{0,1,2:T(4,128)(2,1)S(1)}, u32[]{:S(2)}) copy-start(bf16[64,3,384]{0,1,2:T(4,128)(2,1)S(1)} %copy.46) | copy-start | bytes 442372
  347.6 17.7 %copy-start.2 = (bf16[64,3,384]{0,1,2:T(4,128)(2,1)}, bf16[64,3,384]{0,1,2:T(4,128)(2,1)S(1)}, u32[]{:S(2)}) copy-start(bf16[64,3,384]{0,1,2:T(4,128)(2,1)S(1)} %copy.44) | copy-start | bytes 442372
  379.5 4.0 %copy-start.7 = (bf16[384,512]{1,0:T(8,128)(2,1)S(1)}, bf16[384,512]{1,0:T(8,128)(2,1)}, u32[]{:S(2)}) copy-start(bf16[384,512]{1,0:T(8,128)(2,1)} %constant.63) | copy-start | bytes 1179652
  383.5 2.8 copy-start
  383.5 2.8 copy-start.6
Sparse Core Ops, SparseCore 0:
  321.6 41.0 reduce-scatter.1
where the time goes:
time: 400 us; the launch traced here: 396 us
  blocking collectives  292 us (73%)
  waiting for transfers between devices  36.6 us (9%)
  matrix products  19.4 us (5%)
  between operations  19.4 us (5%)
  local copies, waits for them, and re-layouts  16.8 us (4%)
  starting transfers between devices  11.6 us (3%)
    psum x1, blocking collectives, on_device(): summed_all = lax.psum(picked, 'chan')  266 us
    all_gather x1, blocking collectives, on_device(): receivers = lax.all_gather(spectra, 'src', axis=0, tiled=True)  25.5 us
    all_to_all x1, waiting for transfers between devices, on_device(): lax.all_to_all(strain, 'chan', split_axis=0, concat_axis=1, tiled=True)  21.5 us
    reduce_scatter x1, waiting for transfers between devices, on_device(): lax.psum_scatter(summed_all.astype(jnp.bfloat16), 'src', scatter_dimensio...  15 us
    all_to_all x1, starting transfers between devices, on_device(): lax.all_to_all(strain, 'chan', split_axis=0, concat_axis=1, tiled=True)  11.6 us
  transfers between devices with their start and end apart: 2, of which 2 were waited for; matrix products, arithmetic and copies ran while one was open for 0% of the time, Pallas kernels for 0%

commit v1 on v0

v1 whole, which is shorter than its diff:
```python
import math

import jax
import jax.numpy as jnp
import numpy as np
from jax import lax
from jax.experimental import pallas as pl
from jax.experimental.pallas import tpu as pltpu
from jax.sharding import PartitionSpec as P

DEC = 4
SEG = 7680
NSEG = 3
BIN_LOW = 61
NBIN = 384
NLAG = 512
TAPS = 16
WIN = 31


def taps():
    offsets = np.arange(TAPS)
    centred = (offsets - (TAPS - 1) / 2.0) / DEC
    coeffs = (
        np.sin(np.pi * centred)
        / (np.pi * centred)
        * (0.54 - 0.46 * np.cos(2.0 * np.pi * (offsets + 0.5) / TAPS))
    )
    return coeffs / coeffs.sum()


def band_table(samples, outputs, shift):
    coeffs = taps()
    tap = np.arange(samples)[:, None] + shift - DEC * np.arange(outputs)[None, :]
    inside = (tap >= 0) & (tap < TAPS)
    values = np.where(inside, coeffs[np.clip(tap, 0, TAPS - 1)], 0.0)
    return jnp.asarray(values, jnp.float32).astype(jnp.bfloat16)


def lag_table():
    bin_ids = BIN_LOW + np.arange(NBIN)
    delays = np.arange(NLAG) - NLAG // 2
    angles = 2.0 * np.pi * np.mod(np.outer(bin_ids, delays), SEG) / SEG
    basis = np.concatenate([np.cos(angles), -np.sin(angles)], axis=0) / np.sqrt(NBIN)
    return jnp.asarray(basis, jnp.float32).astype(jnp.bfloat16)


def inner_tables(width):
    bin_ids = BIN_LOW + np.arange(NBIN)
    inner = 2.0 * np.pi * np.mod(np.outer(np.arange(width), bin_ids), SEG) / SEG
    table = jnp.asarray(np.concatenate([np.cos(inner), -np.sin(inner)], axis=1), jnp.float32)
    high = table.astype(jnp.bfloat16)
    low = (table - high.astype(jnp.float32)).astype(jnp.bfloat16)
    return high, low


def outer_tables(width, count):
    bin_ids = BIN_LOW + np.arange(NBIN)
    outer = 2.0 * np.pi * np.mod(np.outer(width * np.arange(count), bin_ids), SEG) / SEG
    return jnp.asarray(np.cos(outer), jnp.float32), jnp.asarray(np.sin(outer), jnp.float32)


def whiten(real_part, imag_part):
    energy = real_part * real_part + imag_part * imag_part
    offsets = np.arange(NBIN)
    band_mask = jnp.asarray((np.abs(offsets[:, None] - offsets[None, :]) <= 32).astype(np.float32))
    smooth = jnp.matmul(energy, band_mask, precision=lax.Precision.HIGHEST) / 65.0
    inverse = lax.rsqrt(smooth + 1e-05)
    return jnp.concatenate([real_part * inverse, imag_part * inverse], axis=-1).astype(jnp.bfloat16)


def correlate_kernel(per_step, src_ref, recv_ref, basis_ref, out_ref, merged):
    rows = recv_ref.shape[1]
    chunk = 16
    for number in range(per_step):
        for low in range(0, rows, chunk):
            total_re = jnp.zeros((chunk, NBIN), jnp.float32)
            total_im = jnp.zeros((chunk, NBIN), jnp.float32)
            for seg in range(NSEG):
                a = src_ref[number, seg : seg + 1, :]
                a_re = a[:, :NBIN]
                a_im = a[:, NBIN:]
                b = recv_ref[seg, low : low + chunk, :].astype(jnp.float32)
                b_re = b[:, :NBIN]
                b_im = b[:, NBIN:]
                total_re += a_re * b_re + a_im * b_im
                total_im += a_re * b_im - a_im * b_re
            spot = number * rows + low
            merged[spot : spot + chunk, :NBIN] = (total_re * (1.0 / NSEG)).astype(jnp.bfloat16)
            merged[spot : spot + chunk, NBIN:] = (total_im * (1.0 / NSEG)).astype(jnp.bfloat16)
    lagged = jnp.dot(merged[...], basis_ref[...], preferred_element_type=jnp.float32)
    out_ref[...] = lagged.astype(jnp.bfloat16)


def correlate(sources, receivers, per_step=4):
    count = sources.shape[0]
    rows = receivers.shape[1]
    return pl.pallas_call(
        lambda *refs: correlate_kernel(per_step, *refs),
        grid=(count // per_step,),
        in_specs=[
            pl.BlockSpec((per_step, NSEG, 2 * NBIN), lambda i: (i, 0, 0)),
            pl.BlockSpec((NSEG, rows, 2 * NBIN), lambda i: (0, 0, 0)),
            pl.BlockSpec((2 * NBIN, NLAG), lambda i: (0, 0)),
        ],
        out_specs=pl.BlockSpec((per_step * rows, NLAG), lambda i: (i, 0)),
        out_shape=jax.ShapeDtypeStruct((count * rows, NLAG), jnp.bfloat16),
        scratch_shapes=[pltpu.VMEM((per_step * rows, 2 * NBIN), jnp.bfloat16)],
        name="correlate",
    )(sources, receivers, lag_table())


def on_device(strain, seg_start, src_chan):
    chan_count = lax.axis_size("chan")
    group_count = lax.axis_size("src")
    local_rows, local_samples = strain.shape
    per_device = local_rows // chan_count
    width = local_samples // DEC
    carried = TAPS - DEC
    carried_out = carried // DEC
    partial_back = jnp.dot(
        strain[:, :carried],
        band_table(carried, carried_out, carried),
        preferred_element_type=jnp.float32,
    )
    partial_back = lax.ppermute(
        partial_back.T.astype(jnp.bfloat16),
        "chan",
        [(number, number - 1) for number in range(1, chan_count)],
    )
    decimated = jnp.dot(
        strain, band_table(local_samples, width, 0), preferred_element_type=jnp.float32
    )
    decimated = decimated + jnp.pad(
        partial_back.T.astype(jnp.float32), ((0, 0), (width - carried_out, 0))
    )
    decimated = decimated.astype(jnp.bfloat16)
    plane_channels = lax.axis_index("src") * local_rows + lax.iota(jnp.int32, local_rows)
    selector = (src_chan[:, None] == plane_channels[None, :]).astype(jnp.bfloat16)
    picked = jnp.dot(selector, decimated, preferred_element_type=jnp.float32).astype(jnp.bfloat16)
    picked = picked.reshape(group_count, -1, width)
    pieces = lax.all_to_all(picked, "src", split_axis=0, concat_axis=0, tiled=True)
    own = jnp.sum(pieces.astype(jnp.float32), axis=0).astype(jnp.bfloat16)
    own_count = own.shape[0]
    share = chan_count // own_count
    outgoing = jnp.concatenate(
        [
            decimated.reshape(chan_count, per_device, width),
            jnp.repeat(own, share, axis=0)[:, None, :],
        ],
        axis=1,
    )
    series = lax.all_to_all(outgoing, "chan", split_axis=0, concat_axis=0, tiled=True)
    series = jnp.pad(series, ((0, 1), (0, 0), (0, 0)))
    aligned = seg_start // width
    offset = seg_start - aligned * width
    position = (width * np.arange(WIN)[:, None] + np.arange(width)[None, :])[:, None, :]
    pieces = []
    for number in range(NSEG):
        window = lax.dynamic_slice_in_dim(series, aligned[number], WIN, 0)
        inside = (position >= offset[number]) & (position < offset[number] + SEG)
        pieces.append(jnp.where(inside, window, jnp.zeros((), jnp.bfloat16)))
    flat = jnp.stack(pieces, axis=0).reshape(-1, width)
    high, low = inner_tables(width)
    part = jnp.dot(flat, high, preferred_element_type=jnp.float32)
    part = part + jnp.dot(flat, low, preferred_element_type=jnp.float32)
    part = part.reshape(NSEG, WIN, per_device + 1, 2 * NBIN)
    phase_cos, phase_sin = outer_tables(width, WIN)
    phase_cos = phase_cos[:, None, :]
    phase_sin = phase_sin[:, None, :]
    part_re = part[..., :NBIN]
    part_im = part[..., NBIN:]
    scale = 1.0 / math.sqrt(SEG)
    total_re = jnp.sum(part_re * phase_cos + part_im * phase_sin, axis=1) * scale
    total_im = jnp.sum(part_im * phase_cos - part_re * phase_sin, axis=1) * scale
    spectra = whiten(total_re, total_im)
    own_recv = spectra[:, :per_device]
    own_src = spectra[:, per_device]
    receivers = lax.all_to_all(
        jnp.broadcast_to(own_recv[None], (group_count,) + own_recv.shape),
        "src",
        split_axis=0,
        concat_axis=0,
        tiled=True,
    )
    receivers = receivers.transpose(1, 0, 2, 3).reshape(NSEG, -1, 2 * NBIN)
    sources = lax.all_to_all(
        jnp.broadcast_to(own_src.reshape(1, -1), (chan_count, own_src.size)),
        "chan",
        split_axis=0,
        concat_axis=0,
        tiled=True,
    )
    sources = sources.reshape(own_count, share, NSEG, 2 * NBIN)[:, 0].astype(jnp.float32)
    lagged = correlate(sources, receivers)
    return lagged.reshape(own_count, group_count, per_device, NLAG)


def solution(mesh):
    return jax.shard_map(
        on_device,
        mesh=mesh,
        in_specs=(P("src", "chan"), P(), P()),
        out_specs=P("src", None, "chan", None),
        check_vma=False,
    )
```

time: 400 us -> 114 us (0.28)
  blocking collectives: 292 us -> 0 us
  starting transfers between devices: 11.6 us -> 35.5 us
  matrix products: 19.4 us -> 6.07 us
  between operations: 19.4 us -> 7.71 us
  other arithmetic: 0.37 us -> 11.2 us
  local copies, waits for them, and re-layouts: 16.8 us -> 7.27 us
  Pallas kernels: 0 us -> 8.01 us
    psum x1 -> x0, blocking collectives: 266 us -> none  [on_device(): summed_all = lax.psum(picked, 'chan')]
    all_gather x1 -> x0, blocking collectives: 25.5 us -> none  [on_device(): receivers = lax.all_gather(spectra, 'src', axis=0, tiled=True)]
    all_to_all x1 -> x4, starting transfers between devices: 11.6 us -> 26.7 us  [the longest x1 10.8 us: on_device(): lax.all_to_all(outgoing, 'chan', split_axis=0, concat_axis=0, tiled=True)]
    all_to_all x1 -> x4, waiting for transfers between devices: 21.5 us -> 36.6 us  [the longest x1 11.9 us: on_device(): lax.all_to_all(jnp.broadcast_to(own_src.reshape(1, -1), (chan_count, own_...]
    reduce_scatter x1 -> x0, waiting for transfers between devices: 15 us -> none  [on_device(): lax.psum_scatter(summed_all.astype(jnp.bfloat16), 'src', scatter_dimensio...]
    dot_general x11 -> x5, matrix products: 19 us -> 5.6 us  [the longest x1 1.88 us: on_device(): jnp.dot(strain, band_table(local_samples, width, 0), preferred_element_ty...]
    ppermute x0 -> x1, starting transfers between devices: none -> 8.75 us  [on_device(): lax.ppermute(partial_back.T.astype(jnp.bfloat16), 'chan', [(number, numbe...]
    div x2 -> x0, local copies, waits for them, and re-layouts: 8.1 us -> none  [the longest x1 4.1 us: on_device(): (cross_im - jnp.einsum('ksf,rsf->krf', source_im, recv_re, preferred_elem...]
  transfers between devices with their start and end apart: 2 -> 5, of which waited for: 2 -> 5; matrix products, arithmetic and copies ran while one was open for 0% -> 7% of each run, Pallas kernels for 0% -> 0%
where the time goes in v1:
time: 114 us; the launch traced here: 113 us
  waiting for transfers between devices  37.4 us (33%)
  starting transfers between devices  35.5 us (31%)
  other arithmetic  11.2 us (10%)
  Pallas kernels  8.01 us (7%)
  between operations  7.71 us (7%)
  local copies, waits for them, and re-layouts  7.27 us (6%)
  matrix products  6.07 us (5%)
    all_to_all x1, waiting for transfers between devices, on_device(): lax.all_to_all(jnp.broadcast_to(own_src.reshape(1, -1), (chan_count, own_...  11.9 us
    all_to_all x1, starting transfers between devices, on_device(): lax.all_to_all(outgoing, 'chan', split_axis=0, concat_axis=0, tiled=True)  10.8 us
    all_to_all x1, waiting for transfers between devices, on_device(): lax.all_to_all(jnp.broadcast_to(own_recv[None], (group_count,) + own_recv...  8.91 us
    ppermute x1, starting transfers between devices, on_device(): lax.ppermute(partial_back.T.astype(jnp.bfloat16), 'chan', [(number, numbe...  8.75 us
    all_to_all x1, waiting for transfers between devices, on_device(): lax.all_to_all(picked, 'src', split_axis=0, concat_axis=0, tiled=True)  8.62 us
    pallas_call x1, Pallas kernels, correlate(): pl.pallas_call(lambda *refs: correlate_kernel(per_step, *refs), grid=(cou...  8.01 us
    all_to_all x1, waiting for transfers between devices, on_device(): lax.all_to_all(outgoing, 'chan', split_axis=0, concat_axis=0, tiled=True)  7.2 us
    all_to_all x1, starting transfers between devices, on_device(): lax.all_to_all(picked, 'src', split_axis=0, concat_axis=0, tiled=True)  6.35 us
  transfers between devices with their start and end apart: 5, of which 5 were waited for; matrix products, arithmetic and copies ran while one was open for 7% of the time, Pallas kernels for 0%

profile of v1, /device:TPU:1, one launch (start us, length us, event | category | flops | bytes accessed | tf_op | source)
XLA Modules:
  0.0 113.1 jit_solution(7566764574198060901)
XLA Ops:
  0.0 1.1 convolution_convert_fusion.1
  1.1 8.8 %collective-permute-start = (bf16[3,512]{1,0:T(4,128)(2,1)S(1)}, bf16[3,512]{1,0:T(4,128)(2,1)S(1)}, u32[]{:S(2)}, u32[]{:S(2)}) collective-permute-start(bf16[3,512]{1,0:T(4,128)(2,1)S(1)} %convolution_convert_fusion.1), channel_id=1, source_target_pairs={{8,0},{16,8},{24,16},{32,24},{40,32},{48,40},{56,48},{64,56},{72,6... | collective-permute-start | bytes 9224 | tf_op jit(solution)/shard_map/ppermute | solution.py:126
  9.9 0.8 collective-permute-done
  10.7 1.9 %add_convert_fusion = bf16[512,256]{0,1:T(8,128)(2,1)S(1)} fusion(bf16[512,3]{0,1:T(4,128)(2,1)S(1)} %bitcast.47, bf16[1024,256]{1,0:T(8,128)(2,1)} %constant.72, bf16[512,1024]{1,0:T(8,128)(2,1)} %param.11), kind=kOutput, calls=%fused_computation.11 | convolution fusion | flops 268828672 | bytes 1838080 | tf_op jit(solution)/shard_map/dot_general | solution.py:131
  12.6 1.6 %convolution_convert_fusion = bf16[256,256]{1,0:T(8,128)(2,1)} fusion(bf16[512,256]{0,1:T(8,128)(2,1)S(1)} %add_convert_fusion, s32[512]{0:T(512)S(1)} %iota_add_fusion, s32[256]{0:T(256)} %param.13), kind=kOutput, calls=%fused_computation.4 | convolution fusion | flops 67305472 | bytes 396288 | tf_op jit(solution)/shard_map/dot_general | solution.py:140
  14.2 6.3 %all-to-all-start = ((bf16[8,32,256]{2,1,0:T(8,128)(2,1)}), bf16[8,32,256]{2,1,0:T(8,128)(2,1)S(1)}, u32[]{:S(2)}, u32[]{:S(2)}) async-start(bf16[8,32,256]{2,1,0:T(8,128)(2,1)} %bitcast.5), calls=%async_computation | async-start | bytes 262144 | tf_op jit(solution)/shard_map/all_to_all | solution.py:142
  20.7 8.6 %all-to-all-done = bf16[8,32,256]{2,1,0:T(8,128)(2,1)S(1)} async-done(((bf16[8,32,256]{2,1,0:T(8,128)(2,1)}), bf16[8,32,256]{2,1,0:T(8,128)(2,1)S(1)}, u32[]{:S(2)}, u32[]{:S(2)}) %all-to-all-start) | async-done | bytes 131104 | tf_op jit(solution)/shard_map/all_to_all | solution.py:142
  29.4 0.9 pad_maximum_fusion.1
  30.2 10.8 %all-to-all-start.1 = ((bf16[64,9,256]{2,1,0:T(8,128)(2,1)}), bf16[64,9,256]{2,1,0:T(8,128)(2,1)S(1)}, u32[]{:S(2)}, u32[]{:S(2)}) async-start(bf16[64,9,256]{2,1,0:T(8,128)(2,1)} %pad_maximum_fusion.1), calls=%async_computation.1 | async-start | bytes 1048576 | tf_op jit(solution)/shard_map/all_to_all | solution.py:153
  49.3 1.9 %and_bitcast_fusion.2 = (pred[31,256]{1,0:T(8,128)(4,1)S(1)}, pred[31,256]{1,0:T(8,128)(4,1)S(1)}, pred[31,256]{1,0:T(8,128)(4,1)S(1)}) fusion(s32[31,1,256]{2,0,1:T(8,128)S(1)} %copy-done.5, s32[]{:T(128)S(6)} %add.51, s32[]{:T(128)} %bitcast, s32[]{:T(128)S(6)} %add.58, s32[]{:T(128)} %bitcast.12, s32[]{:T(128)S(6)} %add.56, s32[]{:T(128)} %bitcast.8), kind=kLoop, calls=%fused_computation.38 | loop fusion | flops 71424 | bytes 55576 | tf_op jit(solution)/shard_map/jit(_where)/broadcast_in_dim | solution.py:162
  51.2 7.2 %all-to-all-done.1 = bf16[64,9,256]{2,1,0:T(8,128)(2,1)S(1)} async-done(((bf16[64,9,256]{2,1,0:T(8,128)(2,1)}), bf16[64,9,256]{2,1,0:T(8,128)(2,1)S(1)}, u32[]{:S(2)}, u32[]{:S(2)}) %all-to-all-start.1) | async-done | bytes 294944 | tf_op jit(solution)/shard_map/all_to_all | solution.py:153
  60.2 2.4 %reshape.43 = f32[3,31,9,768]{3,2,1,0:T(8,128)} reshape(f32[837,768]{1,0:T(8,128)S(1)} %convolution_add_fusion) | data formatting | bytes 5142528 | tf_op jit(solution)/shard_map/reshape | solution.py:167
  62.7 3.1 %add_reduce_fusion = (f32[3,9,384]{2,1,0:T(8,128)S(1)}, f32[3,9,384]{2,1,0:T(8,128)S(1)}) fusion(f32[3,31,9,768]{3,2,1,0:T(8,128)} %reshape.43, f32[31,384]{1,0:T(8,128)S(1)} %copy-done.4, f32[31,384]{1,0:T(8,128)S(1)} %copy-done.3), kind=kLoop, calls=%fused_computation.1 | loop fusion | flops 2550528 | bytes 2749440 | tf_op jit(solution)/shard_map/reduce_sum | solution.py:174
  66.3 0.7 broadcast_in_dim.58
  67.1 3.4 %all-to-all-start.3 = ((bf16[8,3,8,768]{3,2,1,0:T(8,128)(2,1)}), bf16[8,3,8,768]{3,2,1,0:T(8,128)(2,1)S(1)}, u32[]{:S(2)}, u32[]{:S(2)}) async-start(bf16[8,3,8,768]{3,2,1,0:T(8,128)(2,1)} %broadcast_in_dim.58), calls=%async_computation.3 | async-start | bytes 589824 | tf_op jit(solution)/shard_map/all_to_all | solution.py:179
  71.4 2.4 %reduce.4 = bf16[64,2304]{1,0:T(8,128)(2,1)S(1)} reduce(bf16[64,1,2304]{2,1,0:T(2,128)(2,1)S(1)} %broadcast_in_dim.57, bf16[]{:T(256)} %broadcast.45), dimensions={1}, to_apply=%broadcast_in_dim.57.reduce_sub_computation | reduce | bytes 589826 | tf_op jit(solution)/shard_map/broadcast_in_dim | solution.py:188
  73.8 0.8 reshape.51
  74.6 8.9 %all-to-all-done.3 = bf16[8,3,8,768]{3,2,1,0:T(8,128)(2,1)S(1)} async-done(((bf16[8,3,8,768]{3,2,1,0:T(8,128)(2,1)}), bf16[8,3,8,768]{3,2,1,0:T(8,128)(2,1)S(1)}, u32[]{:S(2)}, u32[]{:S(2)}) %all-to-all-start.3) | async-done | bytes 294944 | tf_op jit(solution)/shard_map/all_to_all | solution.py:179
  83.5 6.1 %all-to-all-start.2 = ((bf16[64,2,1152]{2,1,0:T(2,128)(2,1)}), bf16[64,2,1152]{2,1,0:T(2,128)(2,1)S(1)}, u32[]{:S(2)}, u32[]{:S(2)}) async-start(bf16[64,2,1152]{2,1,0:T(2,128)(2,1)} %reshape.51), calls=%async_computation.2 | async-start | bytes 589824 | tf_op jit(solution)/shard_map/all_to_all | solution.py:187
  89.6 0.7 copy_bitcast_fusion.refs_1_
  90.3 11.9 %all-to-all-done.2 = bf16[64,2,1152]{2,1,0:T(2,128)(2,1)S(1)} async-done(((bf16[64,2,1152]{2,1,0:T(2,128)(2,1)}), bf16[64,2,1152]{2,1,0:T(2,128)(2,1)S(1)}, u32[]{:S(2)}, u32[]{:S(2)}) %all-to-all-start.2) | async-done | bytes 294944 | tf_op jit(solution)/shard_map/all_to_all | solution.py:187
  102.4 1.7 %reduce.2 = bf16[64,2304]{1,0:T(8,128)(2,1)S(1)} reduce(bf16[64,1,2304]{2,1,0:T(2,128)(2,1)S(1)} %reshape.52, bf16[]{:T(256)} %constant.80), dimensions={1}, to_apply=%all_to_all.15.reduce_sub_computation | reduce | bytes 589826 | tf_op jit(solution)/shard_map/all_to_all | solution.py:187
  104.3 0.8 fusion.11.refs_0_
  105.1 8.0 %correlate.1 = bf16[2048,512]{1,0:T(8,128)(2,1)} custom-call(f32[32,3,768]{2,1,0:T(4,128)} %fusion.11.refs_0_, bf16[3,64,768]{2,1,0:T(8,128)(2,1)} %copy_bitcast_fusion.refs_1_, bf16[768,512]{1,0:T(8,128)(2,1)} %constant.78.refs_2_), custom_call_target="tpu_custom_call" | custom-call | tf_op jit(solution)/shard_map/correlate/pallas_call | solution.py:98
  (34 shorter events, 4.4 us)
Async XLA Ops:
  1.1 9.6 %collective-permute-start = (bf16[3,512]{1,0:T(4,128)(2,1)S(1)}, bf16[3,512]{1,0:T(4,128)(2,1)S(1)}, u32[]{:S(2)}, u32[]{:S(2)}) collective-permute-start(bf16[3,512]{1,0:T(4,128)(2,1)S(1)} %convolution_convert_fusion.1), channel_id=1, source_target_pairs={{8,0},{16,8},{24,16},{32,24},{40,32},{48,40},{56,48},{64,56},{72,6... | collective-permute-start | bytes 9224 | tf_op jit(solution)/shard_map/ppermute | solution.py:126
  10.7 30.4 %copy-start.6 = (s32[3]{0:T(128)S(1)}, s32[3]{0:T(128)}, u32[]{:S(2)}) copy-start(s32[3]{0:T(128)} %param.12) | copy-start | bytes 40
  10.7 38.6 %copy-start.5 = (s32[31,1,256]{2,0,1:T(8,128)S(1)}, s32[31,1,256]{2,0,1:T(8,128)}, u32[]{:S(2)}) copy-start(s32[31,1,256]{2,0,1:T(8,128)} %constant.62.clone) | copy-start | bytes 95236
  14.2 15.1 %all-to-all-start = ((bf16[8,32,256]{2,1,0:T(8,128)(2,1)}), bf16[8,32,256]{2,1,0:T(8,128)(2,1)S(1)}, u32[]{:S(2)}, u32[]{:S(2)}) async-start(bf16[8,32,256]{2,1,0:T(8,128)(2,1)} %bitcast.5), calls=%async_computation | async-start | bytes 262144 | tf_op jit(solution)/shard_map/all_to_all | solution.py:142
  30.2 28.1 %all-to-all-start.1 = ((bf16[64,9,256]{2,1,0:T(8,128)(2,1)}), bf16[64,9,256]{2,1,0:T(8,128)(2,1)S(1)}, u32[]{:S(2)}, u32[]{:S(2)}) async-start(bf16[64,9,256]{2,1,0:T(8,128)(2,1)} %pad_maximum_fusion.1), calls=%async_computation.1 | async-start | bytes 1048576 | tf_op jit(solution)/shard_map/all_to_all | solution.py:153
  41.1 17.8 %copy-start.2 = (bf16[256,768]{1,0:T(8,128)(2,1)S(1)}, bf16[256,768]{1,0:T(8,128)(2,1)}, u32[]{:S(2)}) copy-start(bf16[256,768]{1,0:T(8,128)(2,1)} %constant.74) | copy-start | bytes 1179652
  58.7 1.0 copy-start.1
  60.2 2.5 %copy-start.3 = (f32[31,384]{1,0:T(8,128)S(1)}, f32[31,384]{1,0:T(8,128)}, u32[]{:S(2)}) copy-start(f32[31,384]{1,0:T(8,128)} %constant.64.clone) | copy-start | bytes 142852
  60.2 2.5 %copy-start.4 = (f32[31,384]{1,0:T(8,128)S(1)}, f32[31,384]{1,0:T(8,128)}, u32[]{:S(2)}) copy-start(f32[31,384]{1,0:T(8,128)} %constant.65.clone) | copy-start | bytes 142852
  62.7 3.1 %copy-start = (f32[384,384,1]{1,0,2:T(8,128)S(1)}, f32[384,384,1]{1,0,2:T(8,128)}, u32[]{:S(2)}) copy-start(f32[384,384,1]{1,0,2:T(8,128)} %constant.79) | copy-start | bytes 1769476
  67.1 16.4 %all-to-all-start.3 = ((bf16[8,3,8,768]{3,2,1,0:T(8,128)(2,1)}), bf16[8,3,8,768]{3,2,1,0:T(8,128)(2,1)S(1)}, u32[]{:S(2)}, u32[]{:S(2)}) async-start(bf16[8,3,8,768]{3,2,1,0:T(8,128)(2,1)} %broadcast_in_dim.58), calls=%async_computation.3 | async-start | bytes 589824 | tf_op jit(solution)/shard_map/all_to_all | solution.py:179
  83.5 18.7 %all-to-all-start.2 = ((bf16[64,2,1152]{2,1,0:T(2,128)(2,1)}), bf16[64,2,1152]{2,1,0:T(2,128)(2,1)S(1)}, u32[]{:S(2)}, u32[]{:S(2)}) async-start(bf16[64,2,1152]{2,1,0:T(2,128)(2,1)} %reshape.51), calls=%async_computation.2 | async-start | bytes 589824 | tf_op jit(solution)/shard_map/all_to_all | solution.py:187

commit v2 on v1

v2 whole, which is shorter than its diff:
```python
import functools
import math

import jax
import jax.numpy as jnp
import numpy as np
from jax import lax
from jax.experimental import pallas as pl
from jax.experimental.pallas import tpu as pltpu
from jax.sharding import PartitionSpec as P

DEC = 4
SEG = 7680
NSEG = 3
BIN_LOW = 61
NBIN = 384
NLAG = 512
TAPS = 16
WIN = 31
WIDTH = 256

MESH = pl.DeviceIdType.MESH


def taps():
    offsets = np.arange(TAPS)
    centred = (offsets - (TAPS - 1) / 2.0) / DEC
    coeffs = (
        np.sin(np.pi * centred)
        / (np.pi * centred)
        * (0.54 - 0.46 * np.cos(2.0 * np.pi * (offsets + 0.5) / TAPS))
    )
    return coeffs / coeffs.sum()


def band_table(samples, outputs, shift):
    coeffs = taps()
    tap = np.arange(samples)[:, None] + shift - DEC * np.arange(outputs)[None, :]
    inside = (tap >= 0) & (tap < TAPS)
    values = np.where(inside, coeffs[np.clip(tap, 0, TAPS - 1)], 0.0)
    return jnp.asarray(values, jnp.float32).astype(jnp.bfloat16)


def lag_table():
    bin_ids = BIN_LOW + np.arange(NBIN)
    delays = np.arange(NLAG) - NLAG // 2
    angles = 2.0 * np.pi * np.mod(np.outer(bin_ids, delays), SEG) / SEG
    basis = np.concatenate([np.cos(angles), -np.sin(angles)], axis=0) / np.sqrt(NBIN)
    return jnp.asarray(basis, jnp.float32).astype(jnp.bfloat16)


def inner_tables(width):
    bin_ids = BIN_LOW + np.arange(NBIN)
    inner = 2.0 * np.pi * np.mod(np.outer(np.arange(width), bin_ids), SEG) / SEG
    table = jnp.asarray(np.concatenate([np.cos(inner), -np.sin(inner)], axis=1), jnp.float32)
    high = table.astype(jnp.bfloat16)
    low = (table - high.astype(jnp.float32)).astype(jnp.bfloat16)
    return high, low


def outer_tables(width, count):
    bin_ids = BIN_LOW + np.arange(NBIN)
    outer = 2.0 * np.pi * np.mod(np.outer(width * np.arange(count), bin_ids), SEG) / SEG
    return jnp.asarray(np.cos(outer), jnp.float32), jnp.asarray(np.sin(outer), jnp.float32)


def smooth_mask():
    offsets = np.arange(NBIN)
    near = np.abs(offsets[:, None] - offsets[None, :]) <= 32
    return jnp.asarray(near.astype(np.float32)).astype(jnp.bfloat16)


def halo_tables():
    carried = TAPS - DEC
    outs = carried // DEC
    coeffs = taps()
    tap = np.arange(128)[None, :] + carried - DEC * np.arange(16)[:, None]
    inside = (tap >= 0) & (tap < TAPS) & (np.arange(16)[:, None] < outs)
    back = np.where(inside, coeffs[np.clip(tap, 0, TAPS - 1)], 0.0)
    place = np.zeros((16, 128))
    place[np.arange(outs), 128 - outs + np.arange(outs)] = 1.0
    return (
        jnp.asarray(back, jnp.float32).astype(jnp.bfloat16),
        jnp.asarray(place, jnp.float32).astype(jnp.bfloat16),
    )


def spectra_of(series, seg_ref, high_ref, low_ref, cos_ref, sin_ref, mask_ref, windows, result):
    lane = lax.broadcasted_iota(jnp.int32, (8, WIDTH), 1)
    for number in range(NSEG):
        start = seg_ref[number]
        first = lax.shift_right_logical(start, 8)
        offset = lax.bitwise_and(start, 255)
        window = series[pl.ds(first, WIN)].astype(jnp.float32)
        base = number * WIN * 8
        windows[base : base + 8, :] = jnp.where(lane >= offset, window[0], 0.0)
        middle = window[1 : WIN - 1].reshape((WIN - 2) * 8, WIDTH)
        windows[base + 8 : base + (WIN - 1) * 8, :] = middle
        windows[base + (WIN - 1) * 8 : base + WIN * 8, :] = jnp.where(
            lane < offset, window[WIN - 1], 0.0
        )
    flat = windows[...].astype(jnp.bfloat16)
    part = jnp.dot(flat, high_ref[...], preferred_element_type=jnp.float32)
    result[...] = part + jnp.dot(flat, low_ref[...], preferred_element_type=jnp.float32)
    scale = 1.0 / math.sqrt(SEG)
    reals, imags = [], []
    for number in range(NSEG):
        total_re = jnp.zeros((8, NBIN), jnp.float32)
        total_im = jnp.zeros((8, NBIN), jnp.float32)
        for block in range(WIN):
            base = (number * WIN + block) * 8
            part_re = result[base : base + 8, :NBIN]
            part_im = result[base : base + 8, NBIN:]
            phase_cos = cos_ref[block : block + 1, :]
            phase_sin = sin_ref[block : block + 1, :]
            total_re += part_re * phase_cos + part_im * phase_sin
            total_im += part_im * phase_cos - part_re * phase_sin
        reals.append(total_re * scale)
        imags.append(total_im * scale)
    real_part = jnp.concatenate(reals, axis=0)
    imag_part = jnp.concatenate(imags, axis=0)
    energy = real_part * real_part + imag_part * imag_part
    smooth = jnp.zeros((NSEG * 8, NBIN), jnp.float32)
    for _ in range(3):
        piece = energy.astype(jnp.bfloat16)
        smooth += jnp.dot(piece, mask_ref[...], preferred_element_type=jnp.float32)
        energy = energy - piece.astype(jnp.float32)
    inverse = lax.rsqrt(smooth / 65.0 + 1e-05)
    white = jnp.concatenate([real_part * inverse, imag_part * inverse], axis=1)
    return white.reshape(NSEG, 8, 2 * NBIN).astype(jnp.bfloat16)


def front_kernel(
    chan_count,
    group_count,
    seg_ref,
    src_ref,
    strain,
    band,
    back,
    place,
    high,
    low,
    cos_ref,
    sin_ref,
    mask,
    recv_out,
    src_out,
    dec,
    series,
    halo_send,
    halo_recv,
    picks,
    picked,
    tiles,
    src_series,
    white,
    gathered,
    src_white,
    src_gathered,
    windows,
    result,
    send,
    recv,
    send_src_sem,
):
    me = lax.axis_index("chan")
    plane = lax.axis_index("src")
    rows = strain.shape[0]

    barrier = pltpu.get_barrier_semaphore()

    def greet_chan(step, carry):
        peer = lax.rem(me + step, chan_count)
        pl.semaphore_signal(barrier, inc=1, device_id={"chan": peer}, device_id_type=MESH)
        return carry

    def greet_src(step, carry):
        peer = lax.rem(plane + step, group_count)
        pl.semaphore_signal(barrier, inc=1, device_id={"src": peer}, device_id_type=MESH)
        return carry

    lax.fori_loop(1, chan_count, greet_chan, 0)
    lax.fori_loop(1, group_count, greet_src, 0)

    halo_send[...] = lax.dot_general(
        back[...],
        strain[:, :128],
        (((1,), (1,)), ((), ())),
        preferred_element_type=jnp.float32,
    ).astype(jnp.bfloat16)
    decimated = jnp.dot(strain[...], band[...], preferred_element_type=jnp.float32)
    series[chan_count] = jnp.zeros((8, WIDTH), jnp.bfloat16)
    channel = lax.broadcasted_iota(jnp.int32, (src_ref.shape[0], rows), 1) + plane * rows
    selector = (src_ref[...] == channel).astype(jnp.float32).astype(jnp.bfloat16)

    pl.semaphore_wait(barrier, chan_count - 1 + group_count - 1)

    before = lax.rem(me + chan_count - 1, chan_count)
    halo = pltpu.make_async_remote_copy(
        halo_send, halo_recv, send.at[0], recv.at[0], {"chan": before}, MESH
    )
    halo.start()
    halo.wait()
    last = jnp.where(me == chan_count - 1, 0.0, 1.0)
    tail = halo_recv[...].astype(jnp.float32) * last
    tail = jnp.dot(
        tail.T.astype(jnp.bfloat16), place[...], preferred_element_type=jnp.float32
    )
    decimated = jnp.concatenate([decimated[:, :128], decimated[:, 128:] + tail], axis=1)
    dec[...] = decimated.reshape(chan_count, 8, WIDTH).astype(jnp.bfloat16)

    def send_chan(step, carry):
        peer = lax.rem(me + step, chan_count)
        pltpu.make_async_remote_copy(
            dec.at[peer], series.at[me], send.at[1], recv.at[1], {"chan": peer}, MESH
        ).start()
        return carry

    lax.fori_loop(1, chan_count, send_chan, 0)
    series[me] = dec[me]

    chosen = jnp.dot(selector, decimated.astype(jnp.bfloat16), preferred_element_type=jnp.float32)
    picks[...] = chosen.reshape(group_count, -1, WIDTH).astype(jnp.bfloat16)

    def send_picks(step, carry):
        peer = lax.rem(plane + step, group_count)
        pltpu.make_async_remote_copy(
            picks.at[peer], picked.at[plane], send.at[2], recv.at[2], {"src": peer}, MESH
        ).start()
        return carry

    lax.fori_loop(1, group_count, send_picks, 0)
    picked[plane] = picks[plane]
    others = pl.ds(0, group_count - 1)
    pltpu.make_async_remote_copy(
        picks.at[others], picked.at[others], send.at[2], recv.at[2], {"src": plane}, MESH
    ).wait()
    own = picked[0].astype(jnp.float32)
    for number in range(1, group_count):
        own += picked[number].astype(jnp.float32)
    tiles[...] = own.reshape(-1, 8, WIDTH).astype(jnp.bfloat16)

    is_owner = lax.rem(me, 4) == 0
    owner_count = chan_count // 4

    def send_tiles(step, carry):
        peer = lax.rem(me + 4 * step - lax.rem(me, 4) + 4, chan_count)

        @pl.when(peer != me)
        def _():
            pltpu.make_async_remote_copy(
                tiles.at[lax.div(peer, 16)],
                src_series.at[me],
                send.at[3],
                recv.at[3],
                {"chan": peer},
                MESH,
            ).start()

        return carry

    lax.fori_loop(0, owner_count, send_tiles, 0)

    everyone = pl.ds(0, chan_count - 1)
    pltpu.make_async_remote_copy(
        dec.at[everyone], series.at[everyone], send.at[1], recv.at[1], {"chan": me}, MESH
    ).wait()
    white[...] = spectra_of(series, seg_ref, high, low, cos_ref, sin_ref, mask, windows, result)

    def send_white(step, carry):
        peer = lax.rem(plane + step, group_count)
        pltpu.make_async_remote_copy(
            white, gathered.at[plane], send.at[4], recv.at[4], {"src": peer}, MESH
        ).start()
        return carry

    lax.fori_loop(1, group_count, send_white, 0)
    gathered[plane] = white[...]

    column = lax.div(me, 16)
    region = lax.div(lax.rem(me, 16), 4)

    @pl.when(is_owner)
    def _():
        src_series[me] = tiles[column]
        src_series[chan_count] = jnp.zeros((8, WIDTH), jnp.bfloat16)
        pltpu.make_async_remote_copy(
            src_series.at[everyone],
            src_series.at[everyone],
            send.at[3],
            recv.at[3],
            {"chan": me},
            MESH,
        ).wait_recv()
        src_white[...] = spectra_of(
            src_series, seg_ref, high, low, cos_ref, sin_ref, mask, windows, result
        )

        def send_src(step, carry):
            peer = 16 * lax.div(step, 4) + 4 * region + lax.rem(step, 4)

            @pl.when(peer != me)
            def _():
                pltpu.make_async_remote_copy(
                    src_white,
                    src_gathered.at[column],
                    send_src_sem.at[step],
                    recv.at[5],
                    {"chan": peer},
                    MESH,
                ).start()

            return carry

        lax.fori_loop(0, 16, send_src, 0)
        src_gathered[column] = src_white[...]

    pltpu.make_async_remote_copy(
        gathered.at[others], gathered.at[others], send.at[4], recv.at[4], {"src": plane}, MESH
    ).wait()
    recv_out[...] = gathered[...]

    def wait_src(count):
        part = src_gathered.at[pl.ds(0, count)]
        return pltpu.make_async_remote_copy(
            part, part, send.at[4], recv.at[5], {"chan": me}, MESH
        )

    @pl.when(is_owner)
    def _():
        wait_src(3).wait_recv()

        def sent_src(step, carry):
            peer = 16 * lax.div(step, 4) + 4 * region + lax.rem(step, 4)

            @pl.when(peer != me)
            def _():
                pltpu.make_async_remote_copy(
                    src_white,
                    src_gathered.at[column],
                    send_src_sem.at[step],
                    recv.at[5],
                    {"chan": peer},
                    MESH,
                ).wait_send()

            return carry

        lax.fori_loop(0, 16, sent_src, 0)
        sent = tiles_wait(src_series, chan_count, owner_count - 1)
        pltpu.make_async_remote_copy(sent, sent, send.at[3], recv.at[3], {"chan": me}, MESH).wait_send()

    @pl.when(jnp.logical_not(is_owner))
    def _():
        wait_src(4).wait_recv()
        sent = tiles_wait(src_series, chan_count, owner_count)
        pltpu.make_async_remote_copy(sent, sent, send.at[3], recv.at[3], {"chan": me}, MESH).wait_send()

    src_out[...] = src_gathered[...]


def tiles_wait(ref, chan_count, count):
    return ref.at[pl.ds(0, count)]


def front(strain, seg_start, src_chan, chan_count, group_count):
    count = src_chan.shape[0]
    share = count // group_count
    back, place = halo_tables()
    high, low = inner_tables(WIDTH)
    phase_cos, phase_sin = outer_tables(WIDTH, WIN)
    vmem = pl.BlockSpec(memory_space=pltpu.VMEM)
    half = jnp.bfloat16
    return pl.pallas_call(
        functools.partial(front_kernel, chan_count, group_count),
        out_shape=(
            jax.ShapeDtypeStruct((group_count, NSEG, 8, 2 * NBIN), half),
            jax.ShapeDtypeStruct((share // 8, NSEG, 8, 2 * NBIN), half),
        ),
        in_specs=[pl.BlockSpec(memory_space=pltpu.SMEM)] + [vmem] * 10,
        out_specs=(vmem, vmem),
        scratch_shapes=[
            pltpu.VMEM((chan_count, 8, WIDTH), half),
            pltpu.VMEM((chan_count + 1, 8, WIDTH), half),
            pltpu.VMEM((16, strain.shape[0]), half),
            pltpu.VMEM((16, strain.shape[0]), half),
            pltpu.VMEM((group_count, share, WIDTH), half),
            pltpu.VMEM((group_count, share, WIDTH), half),
            pltpu.VMEM((share // 8, 8, WIDTH), half),
            pltpu.VMEM((chan_count + 1, 8, WIDTH), half),
            pltpu.VMEM((NSEG, 8, 2 * NBIN), half),
            pltpu.VMEM((group_count, NSEG, 8, 2 * NBIN), half),
            pltpu.VMEM((NSEG, 8, 2 * NBIN), half),
            pltpu.VMEM((share // 8, NSEG, 8, 2 * NBIN), half),
            pltpu.VMEM((NSEG * WIN * 8, WIDTH), jnp.float32),
            pltpu.VMEM((NSEG * WIN * 8, 2 * NBIN), jnp.float32),
            pltpu.SemaphoreType.DMA((5,)),
            pltpu.SemaphoreType.DMA((6,)),
            pltpu.SemaphoreType.DMA((16,)),
        ],
        compiler_params=pltpu.CompilerParams(
            collective_id=0, has_side_effects=True, vmem_limit_bytes=48 << 20
        ),
        name="front",
    )(
        seg_start,
        src_chan[:, None],
        strain,
        band_table(strain.shape[1], WIDTH, 0),
        back,
        place,
        high,
        low,
        phase_cos,
        phase_sin,
        smooth_mask(),
    )


def correlate_kernel(src_ref, recv_ref, basis_ref, out_ref, merged):
    groups = recv_ref.shape[0]
    rows = groups * 8
    for number in range(8):
        for low in range(0, groups, 2):
            reals, imags = [], []
            for group in (low, low + 1):
                total_re = jnp.zeros((8, NBIN), jnp.float32)
                total_im = jnp.zeros((8, NBIN), jnp.float32)
                for seg in range(NSEG):
                    a = src_ref[0, seg, number : number + 1, :].astype(jnp.float32)
                    a_re = a[:, :NBIN]
                    a_im = a[:, NBIN:]
                    b = recv_ref[group, seg].astype(jnp.float32)
                    b_re = b[:, :NBIN]
                    b_im = b[:, NBIN:]
                    total_re += a_re * b_re + a_im * b_im
                    total_im += a_re * b_im - a_im * b_re
                reals.append(total_re * (1.0 / NSEG))
                imags.append(total_im * (1.0 / NSEG))
            spot = number * rows + low * 8
            merged[spot : spot + 16, :NBIN] = jnp.concatenate(reals, axis=0).astype(jnp.bfloat16)
            merged[spot : spot + 16, NBIN:] = jnp.concatenate(imags, axis=0).astype(jnp.bfloat16)
    lagged = jnp.dot(merged[...], basis_ref[...], preferred_element_type=jnp.float32)
    out_ref[...] = lagged.astype(jnp.bfloat16)


def correlate(sources, receivers):
    tiles = sources.shape[0]
    rows = receivers.shape[0] * 8
    return pl.pallas_call(
        correlate_kernel,
        grid=(tiles,),
        in_specs=[
            pl.BlockSpec((1,) + sources.shape[1:], lambda i: (i, 0, 0, 0)),
            pl.BlockSpec(receivers.shape, lambda i: (0, 0, 0, 0)),
            pl.BlockSpec((2 * NBIN, NLAG), lambda i: (0, 0)),
        ],
        out_specs=pl.BlockSpec((8 * rows, NLAG), lambda i: (i, 0)),
        out_shape=jax.ShapeDtypeStruct((tiles * 8 * rows, NLAG), jnp.bfloat16),
        scratch_shapes=[pltpu.VMEM((8 * rows, 2 * NBIN), jnp.bfloat16)],
        name="correlate",
    )(sources, receivers, lag_table())


def on_device(strain, seg_start, src_chan):
    chan_count = lax.axis_size("chan")
    group_count = lax.axis_size("src")
    receivers, sources = front(strain, seg_start, src_chan, chan_count, group_count)
    lagged = correlate(sources, receivers)
    return lagged.reshape(-1, group_count, 8, NLAG)


def solution(mesh):
    return jax.shard_map(
        on_device,
        mesh=mesh,
        in_specs=(P("src", "chan"), P(), P()),
        out_specs=P("src", None, "chan", None),
        check_vma=False,
    )
```

time: 114 us -> 56.8 us (0.50)
  waiting for transfers between devices: 37.4 us -> 0 us
  Pallas kernels: 8.01 us -> 44.9 us
  starting transfers between devices: 35.5 us -> 0 us
  other arithmetic: 11.2 us -> 0 us
  between operations: 7.71 us -> 0.04 us
  matrix products: 6.07 us -> 0 us
  local copies, waits for them, and re-layouts: 7.27 us -> 11 us
    pallas_call x1 -> x2, Pallas kernels: 8.01 us -> 44.9 us  [the longest x1 37.8 us: front(): pl.pallas_call(functools.partial(front_kernel, chan_count, group_count),...]
    all_to_all x4 -> x0, waiting for transfers between devices: 36.6 us -> none  [the longest x1 11.9 us: on_device(): lax.all_to_all(jnp.broadcast_to(own_src.reshape(1, -1), (chan_count, own_...]
    all_to_all x4 -> x0, starting transfers between devices: 26.7 us -> none  [the longest x1 10.8 us: on_device(): lax.all_to_all(outgoing, 'chan', split_axis=0, concat_axis=0, tiled=True)]
    unnamed x16 -> x24, local copies, waits for them, and re-layouts: 1.34 us -> 10.2 us
    ppermute x1 -> x0, starting transfers between devices: 8.75 us -> none  [on_device(): lax.ppermute(partial_back.T.astype(jnp.bfloat16), 'chan', [(number, numbe...]
    dot_general x6 -> x0, matrix products: 6.07 us -> none  [the longest x1 1.88 us: on_device(): jnp.dot(strain, band_table(local_samples, width, 0), preferred_element_ty...]
    broadcast_in_dim x2 -> x0, other arithmetic: 4.27 us -> none  [the longest x1 2.39 us: on_device(): jnp.broadcast_to(own_src.reshape(1, -1), (chan_count, own_src.size))]
    reshape x4 -> x0, local copies, waits for them, and re-layouts: 3.5 us -> none  [the longest x1 2.45 us: on_device(): part = part.reshape(NSEG, WIN, per_device + 1, 2 * NBIN)]
  transfers between devices with their start and end apart: 5 -> 0, of which waited for: 5 -> 0; matrix products, arithmetic and copies ran while one was open for 7% -> 0% of each run, Pallas kernels for 0% -> 0%
where the time goes in v2:
time: 56.8 us; the launch traced here: 55.9 us
  Pallas kernels  44.9 us (79%)
  local copies, waits for them, and re-layouts  11 us (19%)
    pallas_call x1, Pallas kernels, front(): pl.pallas_call(functools.partial(front_kernel, chan_count, group_count),...  37.8 us
    unnamed x24, local copies, waits for them, and re-layouts  10.2 us
    pallas_call x1, Pallas kernels, correlate(): pl.pallas_call(correlate_kernel, grid=(tiles,), in_specs=[pl.BlockSpec((1...  7.04 us

profile of v2, /device:TPU:1, one launch (start us, length us, event | category | flops | bytes accessed | tf_op | source)
XLA Modules:
  0.0 55.9 jit_solution(8124985564030660602)
XLA Ops:
  0.0 0.8 %copy.12.src_ref = s32[256,1]{1,0:T(8,128)S(1)} copy(s32[256,1]{0,1:T(1,128)} %bitcast.2) | data formatting | bytes 2048 | tf_op jit(solution)/shard_map/broadcast_in_dim | solution.py:408
  0.8 0.0 copy-start
  0.8 1.2 %copy-done = bf16[512,1024]{1,0:T(8,128)(2,1)S(1)} copy-done((bf16[512,1024]{1,0:T(8,128)(2,1)S(1)}, bf16[512,1024]{1,0:T(8,128)(2,1)}, u32[]{:S(2)}) %copy-start) | copy-done | bytes 1048600
  2.0 0.0 copy-start.1
  2.0 1.0 %copy-done.1 = bf16[1024,256]{1,0:T(8,128)(2,1)S(1)} copy-done((bf16[1024,256]{1,0:T(8,128)(2,1)S(1)}, bf16[1024,256]{1,0:T(8,128)(2,1)}, u32[]{:S(2)}) %copy-start.1) | copy-done | bytes 524312
  3.1 0.0 copy-start.2
  3.1 1.0 %copy-done.2 = bf16[256,768]{1,0:T(8,128)(2,1)S(1)} copy-done((bf16[256,768]{1,0:T(8,128)(2,1)S(1)}, bf16[256,768]{1,0:T(8,128)(2,1)}, u32[]{:S(2)}) %copy-start.2) | copy-done | bytes 393240
  4.1 0.0 copy-start.3
  4.1 1.0 %copy-done.3 = bf16[256,768]{1,0:T(8,128)(2,1)S(1)} copy-done((bf16[256,768]{1,0:T(8,128)(2,1)S(1)}, bf16[256,768]{1,0:T(8,128)(2,1)}, u32[]{:S(2)}) %copy-start.3) | copy-done | bytes 393240
  5.1 0.0 copy-start.4
  5.1 1.0 %copy-done.4 = bf16[384,384]{1,0:T(8,128)(2,1)S(1)} copy-done((bf16[384,384]{1,0:T(8,128)(2,1)S(1)}, bf16[384,384]{1,0:T(8,128)(2,1)}, u32[]{:S(2)}) %copy-start.4) | copy-done | bytes 294936
  6.0 0.0 copy-start.7
  6.0 0.8 %copy-done.7 = f32[31,384]{1,0:T(8,128)S(1)} copy-done((f32[31,384]{1,0:T(8,128)S(1)}, f32[31,384]{1,0:T(8,128)}, u32[]{:S(2)}) %copy-start.7) | copy-done | bytes 47640
  6.8 0.0 copy-start.8
  6.8 0.8 %copy-done.8 = f32[31,384]{1,0:T(8,128)S(1)} copy-done((f32[31,384]{1,0:T(8,128)S(1)}, f32[31,384]{1,0:T(8,128)}, u32[]{:S(2)}) %copy-start.8) | copy-done | bytes 47640
  7.6 0.0 copy-start.9
  7.6 0.7 %copy-done.9 = bf16[16,128]{1,0:T(8,128)(2,1)S(1)} copy-done((bf16[16,128]{1,0:T(8,128)(2,1)S(1)}, bf16[16,128]{1,0:T(8,128)(2,1)}, u32[]{:S(2)}) %copy-start.9) | copy-done | bytes 4120
  8.3 0.7 %copy-done.10 = bf16[16,128]{1,0:T(8,128)(2,1)S(1)} copy-done((bf16[16,128]{1,0:T(8,128)(2,1)S(1)}, bf16[16,128]{1,0:T(8,128)(2,1)}, u32[]{:S(2)}) %copy-start.10) | copy-done | bytes 4120
  9.0 0.7 %copy-done.11 = s32[3]{0:T(128)S(1)} copy-done((s32[3]{0:T(128)S(1)}, s32[3]{0:T(128)}, u32[]{:S(2)}) %copy-start.11) | copy-done | bytes 36
  9.7 37.8 %front.1 = (bf16[8,3,8,768]{3,2,1,0:T(8,128)(2,1)S(1)}, bf16[4,3,8,768]{3,2,1,0:T(8,128)(2,1)S(1)}) custom-call(s32[3]{0:T(128)S(1)} %copy-done.11, s32[256,1]{1,0:T(8,128)S(1)} %copy.12.src_ref, bf16[512,1024]{1,0:T(8,128)(2,1)S(1)} %copy-done, bf16[1024,256]{1,0:T(8,128)(2,1)S(1)} %copy-done.1, bf16[16,128]{1,0:T(8,128)(2,1)S(1)} %copy-done.10, ...), custom_call_target="tpu_custom_call" | custom-call | tf_op jit(solution)/shard_map/front/pallas_call | solution.py:375
  47.5 0.0 copy-start.5
  47.5 0.7 %copy-done.5 = bf16[8,3,8,768]{3,2,1,0:T(8,128)(2,1)} copy-done((bf16[8,3,8,768]{3,2,1,0:T(8,128)(2,1)}, bf16[8,3,8,768]{3,2,1,0:T(8,128)(2,1)S(1)}, u32[]{:S(2)}) %copy-start.5) | copy-done | bytes 294936
  48.2 0.7 %copy-done.6 = bf16[4,3,8,768]{3,2,1,0:T(8,128)(2,1)} copy-done((bf16[4,3,8,768]{3,2,1,0:T(8,128)(2,1)}, bf16[4,3,8,768]{3,2,1,0:T(8,128)(2,1)S(1)}, u32[]{:S(2)}) %copy-start.6) | copy-done | bytes 147480
  48.9 7.0 %correlate.1 = bf16[2048,512]{1,0:T(8,128)(2,1)} custom-call(bf16[4,3,8,768]{3,2,1,0:T(8,128)(2,1)} %copy-done.6, bf16[8,3,8,768]{3,2,1,0:T(8,128)(2,1)} %copy-done.5, bf16[768,512]{1,0:T(8,128)(2,1)} %constant.32.basis_ref), custom_call_target="tpu_custom_call" | custom-call | tf_op jit(solution)/shard_map/correlate/pallas_call | solution.py:451
  (3 shorter events, 0.0 us)
Async XLA Ops:
  0.8 1.2 %copy-start = (bf16[512,1024]{1,0:T(8,128)(2,1)S(1)}, bf16[512,1024]{1,0:T(8,128)(2,1)}, u32[]{:S(2)}) copy-start(bf16[512,1024]{1,0:T(8,128)(2,1)} %strain.1) | copy-start | bytes 3145732
  2.0 1.0 %copy-start.1 = (bf16[1024,256]{1,0:T(8,128)(2,1)S(1)}, bf16[1024,256]{1,0:T(8,128)(2,1)}, u32[]{:S(2)}) copy-start(bf16[1024,256]{1,0:T(8,128)(2,1)} %constant.24.band) | copy-start | bytes 1572868
  3.1 1.0 %copy-start.2 = (bf16[256,768]{1,0:T(8,128)(2,1)S(1)}, bf16[256,768]{1,0:T(8,128)(2,1)}, u32[]{:S(2)}) copy-start(bf16[256,768]{1,0:T(8,128)(2,1)} %constant.30.low) | copy-start | bytes 1179652
  4.1 1.0 %copy-start.3 = (bf16[256,768]{1,0:T(8,128)(2,1)S(1)}, bf16[256,768]{1,0:T(8,128)(2,1)}, u32[]{:S(2)}) copy-start(bf16[256,768]{1,0:T(8,128)(2,1)} %constant.27.high) | copy-start | bytes 1179652
  5.1 1.0 %copy-start.4 = (bf16[384,384]{1,0:T(8,128)(2,1)S(1)}, bf16[384,384]{1,0:T(8,128)(2,1)}, u32[]{:S(2)}) copy-start(bf16[384,384]{1,0:T(8,128)(2,1)} %constant.31.mask) | copy-start | bytes 884740
  6.0 0.8 %copy-start.7 = (f32[31,384]{1,0:T(8,128)S(1)}, f32[31,384]{1,0:T(8,128)}, u32[]{:S(2)}) copy-start(f32[31,384]{1,0:T(8,128)} %constant.20.clone.sin_ref) | copy-start | bytes 142852
  6.8 0.8 %copy-start.8 = (f32[31,384]{1,0:T(8,128)S(1)}, f32[31,384]{1,0:T(8,128)}, u32[]{:S(2)}) copy-start(f32[31,384]{1,0:T(8,128)} %constant.19.clone.cos_ref) | copy-start | bytes 142852
  7.6 0.7 %copy-start.9 = (bf16[16,128]{1,0:T(8,128)(2,1)S(1)}, bf16[16,128]{1,0:T(8,128)(2,1)}, u32[]{:S(2)}) copy-start(bf16[16,128]{1,0:T(8,128)(2,1)} %constant.26.place) | copy-start | bytes 12292
  8.3 0.7 %copy-start.10 = (bf16[16,128]{1,0:T(8,128)(2,1)S(1)}, bf16[16,128]{1,0:T(8,128)(2,1)}, u32[]{:S(2)}) copy-start(bf16[16,128]{1,0:T(8,128)(2,1)} %constant.25.back) | copy-start | bytes 12292
  9.0 0.7 %copy-start.11 = (s32[3]{0:T(128)S(1)}, s32[3]{0:T(128)}, u32[]{:S(2)}) copy-start(s32[3]{0:T(128)} %seg_ref.1) | copy-start | bytes 40
  47.5 0.7 %copy-start.5 = (bf16[8,3,8,768]{3,2,1,0:T(8,128)(2,1)}, bf16[8,3,8,768]{3,2,1,0:T(8,128)(2,1)S(1)}, u32[]{:S(2)}) copy-start(bf16[8,3,8,768]{3,2,1,0:T(8,128)(2,1)S(1)} %get-tuple-element.8.recv_ref) | copy-start | bytes 884740
  48.2 0.7 %copy-start.6 = (bf16[4,3,8,768]{3,2,1,0:T(8,128)(2,1)}, bf16[4,3,8,768]{3,2,1,0:T(8,128)(2,1)S(1)}, u32[]{:S(2)}) copy-start(bf16[4,3,8,768]{3,2,1,0:T(8,128)(2,1)S(1)} %get-tuple-element.7.src_ref) | copy-start | bytes 442372

commit v3 on v2

v3 whole, which is shorter than its diff:
```python
import functools
import math

import jax
import jax.numpy as jnp
import numpy as np
from jax import lax
from jax.experimental import pallas as pl
from jax.experimental.pallas import tpu as pltpu
from jax.sharding import PartitionSpec as P

DEC = 4
SEG = 7680
NSEG = 3
BIN_LOW = 61
NBIN = 384
NLAG = 512
TAPS = 16
PERIOD = 30
WIDTH = 256

MESH = pl.DeviceIdType.MESH


def taps():
    offsets = np.arange(TAPS)
    centred = (offsets - (TAPS - 1) / 2.0) / DEC
    coeffs = (
        np.sin(np.pi * centred)
        / (np.pi * centred)
        * (0.54 - 0.46 * np.cos(2.0 * np.pi * (offsets + 0.5) / TAPS))
    )
    return coeffs / coeffs.sum()


def band_table(samples, outputs, shift):
    coeffs = taps()
    tap = np.arange(samples)[:, None] + shift - DEC * np.arange(outputs)[None, :]
    inside = (tap >= 0) & (tap < TAPS)
    values = np.where(inside, coeffs[np.clip(tap, 0, TAPS - 1)], 0.0)
    return jnp.asarray(values, jnp.float32).astype(jnp.bfloat16)


def lag_table():
    bin_ids = BIN_LOW + np.arange(NBIN)
    delays = np.arange(NLAG) - NLAG // 2
    angles = 2.0 * np.pi * np.mod(np.outer(bin_ids, delays), SEG) / SEG
    basis = np.concatenate([np.cos(angles), -np.sin(angles)], axis=0) / np.sqrt(NBIN)
    return jnp.asarray(basis, jnp.float32).astype(jnp.bfloat16)


def inner_tables(width):
    bin_ids = BIN_LOW + np.arange(NBIN)
    inner = 2.0 * np.pi * np.mod(np.outer(np.arange(width), bin_ids), SEG) / SEG
    table = jnp.asarray(np.concatenate([np.cos(inner), -np.sin(inner)], axis=1), jnp.float32)
    high = table.astype(jnp.bfloat16)
    low = (table - high.astype(jnp.float32)).astype(jnp.bfloat16)
    return high, low


def outer_tables(width, count):
    bin_ids = BIN_LOW + np.arange(NBIN)
    outer = 2.0 * np.pi * np.mod(np.outer(width * np.arange(count), bin_ids), SEG) / SEG
    return jnp.asarray(np.cos(outer), jnp.float32), jnp.asarray(np.sin(outer), jnp.float32)


def smooth_mask():
    offsets = np.arange(NBIN)
    near = np.abs(offsets[:, None] - offsets[None, :]) <= 32
    return jnp.asarray(near.astype(np.float32)).astype(jnp.bfloat16)


def halo_tables():
    carried = TAPS - DEC
    outs = carried // DEC
    coeffs = taps()
    tap = np.arange(128)[None, :] + carried - DEC * np.arange(16)[:, None]
    inside = (tap >= 0) & (tap < TAPS) & (np.arange(16)[:, None] < outs)
    back = np.where(inside, coeffs[np.clip(tap, 0, TAPS - 1)], 0.0)
    place = np.zeros((16, 128))
    place[np.arange(outs), 128 - outs + np.arange(outs)] = 1.0
    return (
        jnp.asarray(back, jnp.float32).astype(jnp.bfloat16),
        jnp.asarray(place, jnp.float32).astype(jnp.bfloat16),
    )


def local_series(series):
    half = [
        series[:, part].astype(jnp.float32).reshape(-1, 128) for part in range(WIDTH // 128)
    ]
    return jnp.concatenate(half, axis=1)


def spectra_of(series, seg_ref, high_ref, low_ref, cos_ref, sin_ref, mask_ref, result):
    count = series.shape[0] - 1
    lane = lax.broadcasted_iota(jnp.int32, (8, WIDTH), 1)
    firsts = []
    edges = []
    for number in range(NSEG):
        start = seg_ref[number]
        first = lax.shift_right_logical(start, 8)
        offset = lax.bitwise_and(start, 255)
        opening = local_series(series[pl.ds(first, 1)])
        closing = local_series(series[pl.ds(first + PERIOD, 1)])
        edges.append(jnp.where(lane >= offset, opening, closing))
        firsts.append(first)
    flat = jnp.concatenate([local_series(series[0:count])] + edges, axis=0).astype(jnp.bfloat16)
    part = jnp.dot(flat, high_ref[...], preferred_element_type=jnp.float32)
    part = part + jnp.dot(flat, low_ref[...], preferred_element_type=jnp.float32)

    def turned(base, block):
        part_re = part[base : base + 8, :NBIN]
        part_im = part[base : base + 8, NBIN:]
        phase_cos = cos_ref[pl.ds(block, 1), :]
        phase_sin = sin_ref[pl.ds(block, 1), :]
        real = part_re * phase_cos + part_im * phase_sin
        imag = part_im * phase_cos - part_re * phase_sin
        return jnp.concatenate([real, imag], axis=1)

    for block in range(count):
        result[block] = turned(block * 8, block % PERIOD)
    scale = 1.0 / math.sqrt(SEG)
    totals = []
    for number in range(NSEG):
        first = firsts[number]
        total = turned((count + number) * 8, lax.rem(first, PERIOD))
        for block in range(1, PERIOD):
            total += result[first + block]
        totals.append(total * scale)
    total = jnp.concatenate(totals, axis=0)
    real_part = total[:, :NBIN]
    imag_part = total[:, NBIN:]
    energy = real_part * real_part + imag_part * imag_part
    smooth = jnp.zeros((NSEG * 8, NBIN), jnp.float32)
    for _ in range(2):
        piece = energy.astype(jnp.bfloat16)
        smooth += jnp.dot(piece, mask_ref[...], preferred_element_type=jnp.float32)
        energy = energy - piece.astype(jnp.float32)
    inverse = lax.rsqrt(smooth / 65.0 + 1e-05)
    white = jnp.concatenate([real_part * inverse, imag_part * inverse], axis=1)
    return white.reshape(NSEG, 8, 2 * NBIN).astype(jnp.bfloat16)


def front_kernel(
    chan_count,
    group_count,
    strain_hbm,
    back_hbm,
    band_hbm,
    src_hbm,
    place_hbm,
    high_hbm,
    low_hbm,
    cos_hbm,
    sin_hbm,
    mask_hbm,
    seg_hbm,
    basis_hbm,
    recv_out,
    src_out,
    basis,
    strain,
    back,
    band,
    src_ref,
    place,
    high,
    low,
    cos_ref,
    sin_ref,
    mask,
    seg_ref,
    dec,
    series,
    halo_send,
    halo_recv,
    picks,
    picked,
    tiles,
    src_series,
    white,
    gathered,
    src_white,
    src_gathered,
    result,
    load,
    send,
    recv,
    send_src_sem,
):
    me = lax.axis_index("chan")
    plane = lax.axis_index("src")
    rows = strain.shape[0]
    half = WIDTH // 2

    loads = [
        pltpu.make_async_copy(source, target, load.at[number])
        for number, (source, target) in enumerate(
            (
                (strain_hbm, strain),
                (back_hbm, back),
                (band_hbm, band),
                (src_hbm, src_ref),
                (place_hbm, place),
                (high_hbm, high),
                (low_hbm, low),
                (cos_hbm, cos_ref),
                (sin_hbm, sin_ref),
                (mask_hbm, mask),
                (seg_hbm, seg_ref),
                (basis_hbm, basis),
            )
        )
    ]
    for copy in loads[:4]:
        copy.start()

    barrier = pltpu.get_barrier_semaphore()

    def greet_chan(step, carry):
        peer = lax.rem(me + step, chan_count)
        pl.semaphore_signal(barrier, inc=1, device_id={"chan": peer}, device_id_type=MESH)
        return carry

    def greet_src(step, carry):
        peer = lax.rem(plane + step, group_count)
        pl.semaphore_signal(barrier, inc=1, device_id={"src": peer}, device_id_type=MESH)
        return carry

    lax.fori_loop(1, chan_count, greet_chan, 0, unroll=7)
    lax.fori_loop(1, group_count, greet_src, 0, unroll=7)
    for copy in loads[4:]:
        copy.start()

    for copy in loads[:4]:
        copy.wait()
    halo_send[...] = lax.dot_general(
        back[...],
        strain[:, :128],
        (((1,), (1,)), ((), ())),
        preferred_element_type=jnp.float32,
    ).astype(jnp.bfloat16)
    decimated = jnp.dot(strain[...], band[...], preferred_element_type=jnp.float32)
    first_half = decimated[:, :half]
    second_half = decimated[:, half:]
    dec[:, 0] = first_half.reshape(chan_count, 8, half).astype(jnp.bfloat16)
    blank = jnp.zeros((WIDTH // 128, 8, 128), jnp.bfloat16)
    series[chan_count] = blank
    src_series[chan_count] = blank
    listed = jnp.broadcast_to(src_ref[...].astype(jnp.float32), (8, src_ref.shape[1]))
    listed = (listed.T[:, :1]).astype(jnp.int32)
    channel = lax.broadcasted_iota(jnp.int32, (src_ref.shape[1], rows), 1) + plane * rows
    selector = (listed == channel).astype(jnp.float32).astype(jnp.bfloat16)

    def pick(part, values):
        chosen = jnp.dot(
            selector, values.astype(jnp.bfloat16), preferred_element_type=jnp.float32
        )
        picks[part] = chosen.reshape(group_count, -1, half).astype(jnp.bfloat16)

    pick(0, first_half)
    for copy in loads[4:]:
        copy.wait()

    pl.semaphore_wait(barrier, chan_count - 1 + group_count - 1)

    before = lax.rem(me + chan_count - 1, chan_count)
    halo = pltpu.make_async_remote_copy(
        halo_send, halo_recv, send.at[0], recv.at[0], {"chan": before}, MESH
    )
    halo.start()

    def send_picks(part):
        def body(step, carry):
            peer = lax.rem(plane + step, group_count)
            pltpu.make_async_remote_copy(
                picks.at[part, peer],
                picked.at[part, plane],
                send.at[1 + part],
                recv.at[1 + part],
                {"src": peer},
                MESH,
            ).start()
            return carry

        lax.fori_loop(1, group_count, body, 0, unroll=7)
        picked[part, plane] = picks[part, plane]

    def send_chan(part):
        def body(step, carry):
            peer = lax.rem(me + step, chan_count)
            pltpu.make_async_remote_copy(
                dec.at[peer, part],
                series.at[me, part],
                send.at[3 + part],
                recv.at[3 + part],
                {"chan": peer},
                MESH,
            ).start()
            return carry

        lax.fori_loop(1, chan_count, body, 0, unroll=7)
        series[me, part] = dec[me, part]

    send_picks(0)
    send_chan(0)
    halo.wait()
    last = jnp.where(me == chan_count - 1, 0.0, 1.0)
    tail = halo_recv[...].astype(jnp.float32) * last
    tail = jnp.dot(
        tail.T.astype(jnp.bfloat16), place[...], preferred_element_type=jnp.float32
    )
    second_half = second_half + tail
    pick(1, second_half)
    send_picks(1)
    dec[:, 1] = second_half.reshape(chan_count, 8, half).astype(jnp.bfloat16)
    send_chan(1)

    others = pl.ds(0, group_count - 1)
    for part in range(2):
        pltpu.make_async_remote_copy(
            picks.at[part, others],
            picked.at[part, others],
            send.at[1 + part],
            recv.at[1 + part],
            {"src": plane},
            MESH,
        ).wait()
        own = picked[part, 0].astype(jnp.float32)
        for number in range(1, group_count):
            own += picked[part, number].astype(jnp.float32)
        tiles[:, part] = own.reshape(-1, 8, half).astype(jnp.bfloat16)

    is_owner = lax.rem(me, 4) == 0
    owner_count = chan_count // 4

    def send_tiles(step, carry):
        peer = lax.rem(me + 4 * step - lax.rem(me, 4) + 4, chan_count)

        @pl.when(peer != me)
        def _():
            pltpu.make_async_remote_copy(
                tiles.at[lax.div(peer, 16)],
                src_series.at[me],
                send.at[5],
                recv.at[5],
                {"chan": peer},
                MESH,
            ).start()

        return carry

    lax.fori_loop(0, owner_count, send_tiles, 0)

    everyone = pl.ds(0, chan_count - 1)
    for part in range(2):
        pltpu.make_async_remote_copy(
            dec.at[everyone, part],
            series.at[everyone, part],
            send.at[3 + part],
            recv.at[3 + part],
            {"chan": me},
            MESH,
        ).wait()
    tables = (high, low, cos_ref, sin_ref, mask, result)
    white[...] = spectra_of(series, seg_ref, *tables)

    def send_white(step, carry):
        peer = lax.rem(plane + step, group_count)
        pltpu.make_async_remote_copy(
            white, gathered.at[plane], send.at[6], recv.at[6], {"src": peer}, MESH
        ).start()
        return carry

    lax.fori_loop(1, group_count, send_white, 0, unroll=7)
    gathered[plane] = white[...]

    column = lax.div(me, 16)
    region = lax.div(lax.rem(me, 16), 4)

    @pl.when(is_owner)
    def _():
        src_series[me] = tiles[column]
        arrived = src_series.at[everyone]
        pltpu.make_async_remote_copy(
            arrived, arrived, send.at[5], recv.at[5], {"chan": me}, MESH
        ).wait_recv()
        src_white[...] = spectra_of(src_series, seg_ref, *tables)

        def send_src(step, carry):
            peer = 16 * lax.div(step, 4) + 4 * region + lax.rem(step, 4)

            @pl.when(peer != me)
            def _():
                pltpu.make_async_remote_copy(
                    src_white,
                    src_gathered.at[column],
                    send_src_sem.at[step],
                    recv.at[7],
                    {"chan": peer},
                    MESH,
                ).start()

            return carry

        lax.fori_loop(0, 16, send_src, 0)
        src_gathered[column] = src_white[...]

    pltpu.make_async_remote_copy(
        gathered.at[others], gathered.at[others], send.at[6], recv.at[6], {"src": plane}, MESH
    ).wait()
    recv_out[...] = gathered[...].astype(jnp.float32)

    def wait_src(count):
        part = src_gathered.at[pl.ds(0, count)]
        pltpu.make_async_remote_copy(
            part, part, send.at[6], recv.at[7], {"chan": me}, MESH
        ).wait_recv()

    def wait_tiles(count):
        part = src_series.at[pl.ds(0, count)]
        pltpu.make_async_remote_copy(
            part, part, send.at[5], recv.at[5], {"chan": me}, MESH
        ).wait_send()

    @pl.when(is_owner)
    def _():
        wait_src(3)

        def sent_src(step, carry):
            peer = 16 * lax.div(step, 4) + 4 * region + lax.rem(step, 4)

            @pl.when(peer != me)
            def _():
                pltpu.make_async_remote_copy(
                    src_white,
                    src_gathered.at[column],
                    send_src_sem.at[step],
                    recv.at[7],
                    {"chan": peer},
                    MESH,
                ).wait_send()

            return carry

        lax.fori_loop(0, 16, sent_src, 0)
        wait_tiles(owner_count - 1)

    @pl.when(jnp.logical_not(is_owner))
    def _():
        wait_src(4)
        wait_tiles(owner_count)

    src_out[...] = src_gathered[...].astype(jnp.float32) * (1.0 / NSEG)


def front(strain, seg_start, src_chan, chan_count, group_count):
    count = src_chan.shape[0]
    share = count // group_count
    back, place = halo_tables()
    high, low = inner_tables(WIDTH)
    phase_cos, phase_sin = outer_tables(WIDTH, PERIOD)
    vmem = pl.BlockSpec(memory_space=pltpu.VMEM)
    half = jnp.bfloat16
    parts = WIDTH // 128
    operands = (
        strain,
        back,
        band_table(strain.shape[1], WIDTH, 0),
        src_chan.reshape(1, count),
        place,
        high,
        low,
        phase_cos,
        phase_sin,
        smooth_mask(),
        seg_start,
        lag_table(),
    )
    block = (parts, 8, 128)
    spectra = (NSEG, 8, 2 * NBIN)
    return pl.pallas_call(
        functools.partial(front_kernel, chan_count, group_count),
        out_shape=(
            jax.ShapeDtypeStruct((group_count,) + spectra, jnp.float32),
            jax.ShapeDtypeStruct((share // 8,) + spectra, jnp.float32),
            jax.ShapeDtypeStruct((2 * NBIN, NLAG), half),
        ),
        in_specs=[pl.BlockSpec(memory_space=pltpu.HBM)] * len(operands),
        out_specs=(vmem, vmem, vmem),
        scratch_shapes=[pltpu.VMEM(value.shape, value.dtype) for value in operands[:-2]]
        + [
            pltpu.SMEM(seg_start.shape, seg_start.dtype),
            pltpu.VMEM((chan_count,) + block, half),
            pltpu.VMEM((chan_count + 1,) + block, half),
            pltpu.VMEM((16, strain.shape[0]), half),
            pltpu.VMEM((16, strain.shape[0]), half),
            pltpu.VMEM((parts, group_count, share, 128), half),
            pltpu.VMEM((parts, group_count, share, 128), half),
            pltpu.VMEM((share // 8,) + block, half),
            pltpu.VMEM((chan_count + 1,) + block, half),
            pltpu.VMEM(spectra, half),
            pltpu.VMEM((group_count,) + spectra, half),
            pltpu.VMEM(spectra, half),
            pltpu.VMEM((share // 8,) + spectra, half),
            pltpu.VMEM((chan_count, 8, 2 * NBIN), jnp.float32),
            pltpu.SemaphoreType.DMA((len(operands),)),
            pltpu.SemaphoreType.DMA((7,)),
            pltpu.SemaphoreType.DMA((8,)),
            pltpu.SemaphoreType.DMA((16,)),
        ],
        compiler_params=pltpu.CompilerParams(
            collective_id=0, has_side_effects=True, vmem_limit_bytes=40 << 20
        ),
        name="front",
    )(*[pltpu.with_memory_space_constraint(value, pltpu.HBM) for value in operands])


def correlate_kernel(src_ref, recv_ref, basis, out_ref, merged, lagged, sems):
    groups = recv_ref.shape[0]
    rows = groups * 8
    per_step = 4
    steps = src_ref.shape[0] * 8 // per_step

    def produce(step):
        for index in range(per_step):
            tile, number = divmod(step * per_step + index, 8)
            for low in range(0, groups, 2):
                reals, imags = [], []
                for group in (low, low + 1):
                    total_re = None
                    for seg in range(NSEG):
                        a_re = src_ref[tile, seg, number : number + 1, :NBIN]
                        a_im = src_ref[tile, seg, number : number + 1, NBIN:]
                        b_re = recv_ref[group, seg, :, :NBIN]
                        b_im = recv_ref[group, seg, :, NBIN:]
                        term_re = a_re * b_re + a_im * b_im
                        term_im = a_re * b_im - a_im * b_re
                        total_re = term_re if total_re is None else total_re + term_re
                        total_im = term_im if seg == 0 else total_im + term_im
                    reals.append(total_re)
                    imags.append(total_im)
                spot = index * rows + low * 8
                merged[step % 2, spot : spot + 16, :NBIN] = jnp.concatenate(
                    reals, axis=0
                ).astype(jnp.bfloat16)
                merged[step % 2, spot : spot + 16, NBIN:] = jnp.concatenate(
                    imags, axis=0
                ).astype(jnp.bfloat16)

    copies = []
    produce(0)
    for step in range(steps):
        values = jnp.dot(merged[step % 2], basis[...], preferred_element_type=jnp.float32)
        if step + 1 < steps:
            produce(step + 1)
        lagged[step] = values.astype(jnp.bfloat16)
        size = per_step * rows
        copy = pltpu.make_async_copy(
            lagged.at[step], out_ref.at[pl.ds(step * size, size)], sems.at[step]
        )
        copy.start()
        copies.append(copy)
    for copy in copies:
        copy.wait()


def correlate(sources, receivers, basis):
    tiles = sources.shape[0]
    rows = receivers.shape[0] * 8
    steps = tiles * 2
    vmem = pl.BlockSpec(memory_space=pltpu.VMEM)
    return pl.pallas_call(
        correlate_kernel,
        in_specs=[vmem, vmem, vmem],
        out_specs=pl.BlockSpec(memory_space=pltpu.HBM),
        out_shape=jax.ShapeDtypeStruct((tiles * 8 * rows, NLAG), jnp.bfloat16),
        scratch_shapes=[
            pltpu.VMEM((2, 4 * rows, 2 * NBIN), jnp.bfloat16),
            pltpu.VMEM((steps, 4 * rows, NLAG), jnp.bfloat16),
            pltpu.SemaphoreType.DMA((steps,)),
        ],
        compiler_params=pltpu.CompilerParams(vmem_limit_bytes=40 << 20),
        name="correlate",
    )(sources, receivers, basis)


def on_device(strain, seg_start, src_chan):
    chan_count = lax.axis_size("chan")
    group_count = lax.axis_size("src")
    receivers, sources, basis = front(strain, seg_start, src_chan, chan_count, group_count)
    lagged = correlate(sources, receivers, basis)
    return lagged.reshape(-1, group_count, 8, NLAG)


def solution(mesh):
    return jax.shard_map(
        on_device,
        mesh=mesh,
        in_specs=(P("src", "chan"), P(), P()),
        out_specs=P("src", None, "chan", None),
        check_vma=False,
    )
```

time: 56.8 us -> 40.7 us (0.72)
  local copies, waits for them, and re-layouts: 11 us -> 0 us
  Pallas kernels: 44.9 us -> 40 us
    unnamed x24 -> x0, local copies, waits for them, and re-layouts: 10.2 us -> none
    pallas_call x1, Pallas kernels: 7.04 us -> 4.54 us  [correlate(): pl.pallas_call(correlate_kernel, in_specs=[vmem, vmem, vmem], out_specs=p...]
    pallas_call x1, Pallas kernels: 37.8 us -> 35.4 us  [front(): pl.pallas_call(functools.partial(front_kernel, chan_count, group_count),...]
    broadcast_in_dim x1 -> x0, local copies, waits for them, and re-layouts: 0.8 us -> none  [front(): src_chan[:, None]]
where the time goes in v3:
time: 40.7 us; the launch traced here: 40 us
  Pallas kernels  40 us (98%)
    pallas_call x1, Pallas kernels, front(): pl.pallas_call(functools.partial(front_kernel, chan_count, group_count),...  35.4 us
    pallas_call x1, Pallas kernels, correlate(): pl.pallas_call(correlate_kernel, in_specs=[vmem, vmem, vmem], out_specs=p...  4.54 us

profile of v3, /device:TPU:1, one launch (start us, length us, event | category | flops | bytes accessed | tf_op | source)
XLA Modules:
  0.0 40.0 jit_solution(936333247957427072)
XLA Ops:
  0.0 35.4 %front.1 = (f32[8,3,8,768]{3,2,1,0:T(8,128)S(1)}, f32[4,3,8,768]{3,2,1,0:T(8,128)S(1)}, bf16[768,512]{1,0:T(8,128)(2,1)S(1)}) custom-call(bf16[512,1024]{1,0:T(8,128)(2,1)} %strain_hbm.1, bf16[16,128]{1,0:T(8,128)(2,1)} %constant.24.back_hbm, bf16[1024,256]{1,0:T(8,128)(2,1)} %constant.25.band_hbm, s32[1,256]{1,0:T(1,128)} %bitcast.2, ...), custom_call_target="tpu_custom_call" | custom-call | tf_op jit(solution)/shard_map/front/pallas_call | solution.py:483
  35.5 4.5 %correlate.1 = bf16[2048,512]{1,0:T(8,128)(2,1)} custom-call(f32[4,3,8,768]{3,2,1,0:T(8,128)S(1)} %get-tuple-element.8.src_ref, f32[8,3,8,768]{3,2,1,0:T(8,128)S(1)} %get-tuple-element.9.recv_ref, bf16[768,512]{1,0:T(8,128)(2,1)S(1)} %get-tuple-element.10.basis), custom_call_target="tpu_custom_call" | custom-call | tf_op jit(solution)/shard_map/correlate/pallas_call | solution.py:574

commit v4 on v3

--- a/solution.py
+++ b/solution.py
@@ -140,6 +140,19 @@
     inverse = lax.rsqrt(smooth / 65.0 + 1e-05)
     white = jnp.concatenate([real_part * inverse, imag_part * inverse], axis=1)
     return white.reshape(NSEG, 8, 2 * NBIN).astype(jnp.bfloat16)
+
+
+def each_group(plane, act):
+    for step in (1, 2, 3, 4, 5, 6, 7):
+        act(lax.rem(plane + step, 8))
+
+
+def each_in_plane(me, act):
+    def body(step, carry):
+        act(lax.rem(me + step, 64))
+        return carry
+
+    lax.fori_loop(1, 64, body, 0, unroll=7)
 
 
 def front_kernel(
@@ -175,6 +188,8 @@
     series,
     halo_send,
     halo_recv,
+    early,
+    early_recv,
     picks,
     picked,
     tiles,
@@ -218,18 +233,20 @@
 
     barrier = pltpu.get_barrier_semaphore()
 
-    def greet_chan(step, carry):
-        peer = lax.rem(me + step, chan_count)
+    def greet_chan(peer):
         pl.semaphore_signal(barrier, inc=1, device_id={"chan": peer}, device_id_type=MESH)
-        return carry
-
-    def greet_src(step, carry):
-        peer = lax.rem(plane + step, group_count)
+
+    before = lax.rem(me + chan_count - 1, chan_count)
+    after = lax.rem(me + 1, chan_count)
+
+    def greet_src(peer):
         pl.semaphore_signal(barrier, inc=1, device_id={"src": peer}, device_id_type=MESH)
-        return carry
-
-    lax.fori_loop(1, chan_count, greet_chan, 0, unroll=7)
-    lax.fori_loop(1, group_count, greet_src, 0, unroll=7)
+        pl.semaphore_signal(
+            barrier, inc=1, device_id={"chan": after, "src": peer}, device_id_type=MESH
+        )
+
+    each_in_plane(me, greet_chan)
+    each_group(plane, greet_src)
     for copy in loads[4:]:
         copy.start()
 
@@ -253,43 +270,49 @@
     channel = lax.broadcasted_iota(jnp.int32, (src_ref.shape[1], rows), 1) + plane * rows
     selector = (listed == channel).astype(jnp.float32).astype(jnp.bfloat16)
 
-    def pick(part, values):
-        chosen = jnp.dot(
-            selector, values.astype(jnp.bfloat16), preferred_element_type=jnp.float32
-        )
-        picks[part] = chosen.reshape(group_count, -1, half).astype(jnp.bfloat16)
-
-    pick(0, first_half)
+    chosen = jnp.dot(selector, decimated.astype(jnp.bfloat16), preferred_element_type=jnp.float32)
+    for part in range(2):
+        piece = chosen[:, part * half : (part + 1) * half].reshape(group_count, -1, half)
+        picks[:, part] = piece.astype(jnp.bfloat16)
+    chosen = lax.dot_general(
+        halo_send[...],
+        selector,
+        (((1,), (1,)), ((), ())),
+        preferred_element_type=jnp.float32,
+    )
+    share = src_ref.shape[1] // group_count
+    for group in range(group_count):
+        place_at = group * share
+        piece = chosen[:, place_at // 128 * 128 : place_at // 128 * 128 + 128]
+        if place_at % 128:
+            piece = pltpu.roll(piece, 128 - place_at % 128, 1)
+        early[group] = piece.astype(jnp.bfloat16)
     for copy in loads[4:]:
         copy.wait()
 
-    pl.semaphore_wait(barrier, chan_count - 1 + group_count - 1)
-
-    before = lax.rem(me + chan_count - 1, chan_count)
+    pl.semaphore_wait(barrier, chan_count - 1 + 2 * (group_count - 1))
+
+    def send_early(peer):
+        pltpu.make_async_remote_copy(
+            early.at[peer],
+            early_recv.at[plane],
+            send.at[1],
+            recv.at[1],
+            {"chan": before, "src": peer},
+            MESH,
+        ).start()
+
     halo = pltpu.make_async_remote_copy(
         halo_send, halo_recv, send.at[0], recv.at[0], {"chan": before}, MESH
     )
-    halo.start()
-
-    def send_picks(part):
-        def body(step, carry):
-            peer = lax.rem(plane + step, group_count)
-            pltpu.make_async_remote_copy(
-                picks.at[part, peer],
-                picked.at[part, plane],
-                send.at[1 + part],
-                recv.at[1 + part],
-                {"src": peer},
-                MESH,
-            ).start()
-            return carry
-
-        lax.fori_loop(1, group_count, body, 0, unroll=7)
-        picked[part, plane] = picks[part, plane]
+
+    def send_picks(peer):
+        pltpu.make_async_remote_copy(
+            picks.at[peer], picked.at[plane], send.at[2], recv.at[2], {"src": peer}, MESH
+        ).start()
 
     def send_chan(part):
-        def body(step, carry):
-            peer = lax.rem(me + step, chan_count)
+        def body(peer):
             pltpu.make_async_remote_copy(
                 dec.at[peer, part],
                 series.at[me, part],
@@ -298,13 +321,16 @@
                 {"chan": peer},
                 MESH,
             ).start()
-            return carry
-
-        lax.fori_loop(1, chan_count, body, 0, unroll=7)
+
+        each_in_plane(me, body)
         series[me, part] = dec[me, part]
 
-    send_picks(0)
+    halo.start()
+    each_group(plane, send_picks)
+    each_group(plane, send_early)
+    send_early(plane)
     send_chan(0)
+    picked[plane] = picks[plane]
     halo.wait()
     last = jnp.where(me == chan_count - 1, 0.0, 1.0)
     tail = halo_recv[...].astype(jnp.float32) * last
@@ -312,46 +338,54 @@
         tail.T.astype(jnp.bfloat16), place[...], preferred_element_type=jnp.float32
     )
     second_half = second_half + tail
-    pick(1, second_half)
-    send_picks(1)
     dec[:, 1] = second_half.reshape(chan_count, 8, half).astype(jnp.bfloat16)
     send_chan(1)
 
     others = pl.ds(0, group_count - 1)
+    pltpu.make_async_remote_copy(
+        early, early_recv, send.at[1], recv.at[1], {"src": plane}, MESH
+    ).wait()
+    tail = early_recv[0].astype(jnp.float32)
+    for number in range(1, group_count):
+        tail += early_recv[number].astype(jnp.float32)
+    tail = jnp.dot(
+        (tail * last).T[:share].astype(jnp.bfloat16), place[...], preferred_element_type=jnp.float32
+    )
+    pltpu.make_async_remote_copy(
+        picks.at[others], picked.at[others], send.at[2], recv.at[2], {"src": plane}, MESH
+    ).wait()
     for part in range(2):
-        pltpu.make_async_remote_copy(
-            picks.at[part, others],
-            picked.at[part, others],
-            send.at[1 + part],
-            recv.at[1 + part],
-            {"src": plane},
-            MESH,
-        ).wait()
-        own = picked[part, 0].astype(jnp.float32)
+        own = picked[0, part].astype(jnp.float32)
         for number in range(1, group_count):
-            own += picked[part, number].astype(jnp.float32)
+            own += picked[number, part].astype(jnp.float32)
+        if part == 1:
+            own += tail
         tiles[:, part] = own.reshape(-1, 8, half).astype(jnp.bfloat16)
 
+    column = lax.div(me, 16)
+    row = lax.div(lax.rem(me, 16), 2)
+    region = lax.div(row, 2)
     is_owner = lax.rem(me, 4) == 0
     owner_count = chan_count // 4
-
-    def send_tiles(step, carry):
-        peer = lax.rem(me + 4 * step - lax.rem(me, 4) + 4, chan_count)
-
-        @pl.when(peer != me)
-        def _():
-            pltpu.make_async_remote_copy(
-                tiles.at[lax.div(peer, 16)],
-                src_series.at[me],
-                send.at[5],
-                recv.at[5],
-                {"chan": peer},
-                MESH,
-            ).start()
-
-        return carry
-
-    lax.fori_loop(0, owner_count, send_tiles, 0)
+    for step in (2, 1, 3, 0):
+        for side in (2, 1, 3, 0):
+            tile = lax.rem(column + side, 4)
+            peer = 16 * tile + 4 * lax.rem(region + step, 4)
+
+            def send_tile(tile=tile, peer=peer):
+                pltpu.make_async_remote_copy(
+                    tiles.at[tile],
+                    src_series.at[me],
+                    send.at[5],
+                    recv.at[5],
+                    {"chan": peer},
+                    MESH,
+                ).start()
+
+            if step == 0 and side == 0:
+                pl.when(jnp.logical_not(is_owner))(send_tile)
+            else:
+                send_tile()
 
     everyone = pl.ds(0, chan_count - 1)
     for part in range(2):
@@ -366,18 +400,46 @@
     tables = (high, low, cos_ref, sin_ref, mask, result)
     white[...] = spectra_of(series, seg_ref, *tables)
 
-    def send_white(step, carry):
+    turn = 1 - 2 * lax.rem(me, 2)
+    for step in (3, 5, 2, 6, 1, 7):
+        distance = step if step < 4 else step - 8
         peer = lax.rem(plane + step, group_count)
-        pltpu.make_async_remote_copy(
-            white, gathered.at[plane], send.at[6], recv.at[6], {"src": peer}, MESH
+        number = jnp.where(turn * 3 == distance, 8, 6) if step in (3, 5) else 6
+        pltpu.make_async_remote_copy(
+            white, gathered.at[plane], send.at[6], recv.at[number], {"src": peer}, MESH
         ).start()
-        return carry
-
-    lax.fori_loop(1, group_count, send_white, 0, unroll=7)
     gathered[plane] = white[...]
 
-    column = lax.div(me, 16)
-    region = lax.div(lax.rem(me, 16), 4)
+    def source_copy(number):
+        side, place = divmod(number, 4)
+        side = (2, 1, 3, 0)[side]
+        other = lax.rem(lax.rem(me, 4) + 3 - place, 4)
+        peer = 16 * lax.rem(column + side, 4) + 4 * region + other
+        return pltpu.make_async_remote_copy(
+            src_white,
+            src_gathered.at[column],
+            send_src_sem.at[number],
+            recv.at[7],
+            {"chan": peer},
+            MESH,
+        )
+
+    passed = lax.rem(plane + group_count - 3 * turn, group_count)
+    onward = lax.rem(plane + group_count + turn, group_count)
+    forward = pltpu.make_async_remote_copy(
+        gathered.at[passed],
+        gathered.at[passed],
+        send.at[7],
+        recv.at[6],
+        {"src": onward},
+        MESH,
+    )
+
+    def pass_on():
+        pltpu.make_async_remote_copy(
+            white, gathered.at[passed], send.at[7], recv.at[8], {"src": onward}, MESH
+        ).wait_recv()
+        forward.start()
 
     @pl.when(is_owner)
     def _():
@@ -388,28 +450,20 @@
         ).wait_recv()
         src_white[...] = spectra_of(src_series, seg_ref, *tables)
 
-        def send_src(step, carry):
-            peer = 16 * lax.div(step, 4) + 4 * region + lax.rem(step, 4)
-
-            @pl.when(peer != me)
-            def _():
-                pltpu.make_async_remote_copy(
-                    src_white,
-                    src_gathered.at[column],
-                    send_src_sem.at[step],
-                    recv.at[7],
-                    {"chan": peer},
-                    MESH,
-                ).start()
-
-            return carry
-
-        lax.fori_loop(0, 16, send_src, 0)
+        for number in range(15):
+            source_copy(number).start()
+        pass_on()
         src_gathered[column] = src_white[...]
 
+    @pl.when(jnp.logical_not(is_owner))
+    def _():
+        pass_on()
+
+    most = gathered.at[pl.ds(0, group_count - 2)]
     pltpu.make_async_remote_copy(
-        gathered.at[others], gathered.at[others], send.at[6], recv.at[6], {"src": plane}, MESH
+        most, most, send.at[6], recv.at[6], {"src": plane}, MESH
     ).wait()
+    forward.wait_send()
     recv_out[...] = gathered[...].astype(jnp.float32)
 
     def wait_src(count):
@@ -428,23 +482,8 @@
     def _():
         wait_src(3)
 
-        def sent_src(step, carry):
-            peer = 16 * lax.div(step, 4) + 4 * region + lax.rem(step, 4)
-
-            @pl.when(peer != me)
-            def _():
-                pltpu.make_async_remote_copy(
-                    src_white,
-                    src_gathered.at[column],
-                    send_src_sem.at[step],
-                    recv.at[7],
-                    {"chan": peer},
-                    MESH,
-                ).wait_send()
-
-            return carry
-
-        lax.fori_loop(0, 16, sent_src, 0)
+        for number in range(15):
+            source_copy(number).wait_send()
         wait_tiles(owner_count - 1)
 
     @pl.when(jnp.logical_not(is_owner))
@@ -496,8 +535,10 @@
             pltpu.VMEM((chan_count + 1,) + block, half),
             pltpu.VMEM((16, strain.shape[0]), half),
             pltpu.VMEM((16, strain.shape[0]), half),
-            pltpu.VMEM((parts, group_count, share, 128), half),
-            pltpu.VMEM((parts, group_count, share, 128), half),
+            pltpu.VMEM((group_count, 16, 128), half),
+            pltpu.VMEM((group_count, 16, 128), half),
+            pltpu.VMEM((group_count, parts, share, 128), half),
+            pltpu.VMEM((group_count, parts, share, 128), half),
             pltpu.VMEM((share // 8,) + block, half),
             pltpu.VMEM((chan_count + 1,) + block, half),
             pltpu.VMEM(spectra, half),
@@ -506,9 +547,9 @@
             pltpu.VMEM((share // 8,) + spectra, half),
             pltpu.VMEM((chan_count, 8, 2 * NBIN), jnp.float32),
             pltpu.SemaphoreType.DMA((len(operands),)),
-            pltpu.SemaphoreType.DMA((7,)),
             pltpu.SemaphoreType.DMA((8,)),
-            pltpu.SemaphoreType.DMA((16,)),
+            pltpu.SemaphoreType.DMA((9,)),
+            pltpu.SemaphoreType.DMA((15,)),
         ],
         compiler_params=pltpu.CompilerParams(
             collective_id=0, has_side_effects=True, vmem_limit_bytes=40 << 20

time: 40.7 us -> 39.9 us (0.980); the launches traced: 40 us -> 39.7 us
  no operation moved by 1% of the time
where the time goes in v4:
time: 39.9 us; the launch traced here: 39.7 us
  Pallas kernels  39.7 us (99%)
    pallas_call x1, Pallas kernels, front(): pl.pallas_call(functools.partial(front_kernel, chan_count, group_count),...  35.2 us
    pallas_call x1, Pallas kernels, correlate(): pl.pallas_call(correlate_kernel, in_specs=[vmem, vmem, vmem], out_specs=p...  4.54 us

profile of v4, /device:TPU:1, one launch (start us, length us, event | category | flops | bytes accessed | tf_op | source)
XLA Modules:
  0.0 39.7 jit_solution(2279265494557746182)
XLA Ops:
  0.0 35.2 %front.1 = (f32[8,3,8,768]{3,2,1,0:T(8,128)S(1)}, f32[4,3,8,768]{3,2,1,0:T(8,128)S(1)}, bf16[768,512]{1,0:T(8,128)(2,1)S(1)}) custom-call(bf16[512,1024]{1,0:T(8,128)(2,1)} %strain_hbm.1, bf16[16,128]{1,0:T(8,128)(2,1)} %constant.24.back_hbm, bf16[1024,256]{1,0:T(8,128)(2,1)} %constant.25.band_hbm, s32[1,256]{1,0:T(1,128)} %bitcast.2, ...), custom_call_target="tpu_custom_call" | custom-call | tf_op jit(solution)/shard_map/front/pallas_call | solution.py:522
  35.2 4.5 %correlate.1 = bf16[2048,512]{1,0:T(8,128)(2,1)} custom-call(f32[4,3,8,768]{3,2,1,0:T(8,128)S(1)} %get-tuple-element.8.src_ref, f32[8,3,8,768]{3,2,1,0:T(8,128)S(1)} %get-tuple-element.9.recv_ref, bf16[768,512]{1,0:T(8,128)(2,1)S(1)} %get-tuple-element.10.basis), custom_call_target="tpu_custom_call" | custom-call | tf_op jit(solution)/shard_map/correlate/pallas_call | solution.py:615

commit v5 on v4

--- a/solution.py
+++ b/solution.py
@@ -464,7 +464,9 @@
         most, most, send.at[6], recv.at[6], {"src": plane}, MESH
     ).wait()
     forward.wait_send()
-    recv_out[...] = gathered[...].astype(jnp.float32)
+    for pair in range(group_count // 2):
+        both = [gathered[2 * pair + side].astype(jnp.float32) for side in range(2)]
+        recv_out[pair] = jnp.concatenate(both, axis=1).astype(jnp.bfloat16)
 
     def wait_src(count):
         part = src_gathered.at[pl.ds(0, count)]
@@ -491,7 +493,7 @@
         wait_src(4)
         wait_tiles(owner_count)
 
-    src_out[...] = src_gathered[...].astype(jnp.float32) * (1.0 / NSEG)
+    src_out[...] = src_gathered[...].astype(jnp.float32)
 
 
 def front(strain, seg_start, src_chan, chan_count, group_count):
@@ -522,7 +524,7 @@
     return pl.pallas_call(
         functools.partial(front_kernel, chan_count, group_count),
         out_shape=(
-            jax.ShapeDtypeStruct((group_count,) + spectra, jnp.float32),
+            jax.ShapeDtypeStruct((group_count // 2, NSEG, 16, 2 * NBIN), half),
             jax.ShapeDtypeStruct((share // 8,) + spectra, jnp.float32),
             jax.ShapeDtypeStruct((2 * NBIN, NLAG), half),
         ),
@@ -559,36 +561,34 @@
 
 
 def correlate_kernel(src_ref, recv_ref, basis, out_ref, merged, lagged, sems):
-    groups = recv_ref.shape[0]
-    rows = groups * 8
+    pairs = recv_ref.shape[0]
+    rows = pairs * 16
     per_step = 4
     steps = src_ref.shape[0] * 8 // per_step
 
     def produce(step):
         for index in range(per_step):
             tile, number = divmod(step * per_step + index, 8)
-            for low in range(0, groups, 2):
-                reals, imags = [], []
-                for group in (low, low + 1):
-                    total_re = None
-                    for seg in range(NSEG):
-                        a_re = src_ref[tile, seg, number : number + 1, :NBIN]
-                        a_im = src_ref[tile, seg, number : number + 1, NBIN:]
-                        b_re = recv_ref[group, seg, :, :NBIN]
-                        b_im = recv_ref[group, seg, :, NBIN:]
-                        term_re = a_re * b_re + a_im * b_im
-                        term_im = a_re * b_im - a_im * b_re
-                        total_re = term_re if total_re is None else total_re + term_re
-                        total_im = term_im if seg == 0 else total_im + term_im
-                    reals.append(total_re)
-                    imags.append(total_im)
-                spot = index * rows + low * 8
-                merged[step % 2, spot : spot + 16, :NBIN] = jnp.concatenate(
-                    reals, axis=0
+            source = [
+                jnp.broadcast_to(
+                    src_ref[tile, seg, number : number + 1, :], (16, 2 * NBIN)
                 ).astype(jnp.bfloat16)
-                merged[step % 2, spot : spot + 16, NBIN:] = jnp.concatenate(
-                    imags, axis=0
-                ).astype(jnp.bfloat16)
+                for seg in range(NSEG)
+            ]
+            for pair in range(pairs):
+                total_re = total_im = None
+                for seg in range(NSEG):
+                    a_re = source[seg][:, :NBIN]
+                    a_im = source[seg][:, NBIN:]
+                    b_re = recv_ref[pair, seg, :, :NBIN]
+                    b_im = recv_ref[pair, seg, :, NBIN:]
+                    term_re = a_re * b_re + a_im * b_im
+                    term_im = a_re * b_im - a_im * b_re
+                    total_re = term_re if seg == 0 else total_re + term_re
+                    total_im = term_im if seg == 0 else total_im + term_im
+                spot = index * rows + pair * 16
+                merged[step % 2, spot : spot + 16, :NBIN] = total_re
+                merged[step % 2, spot : spot + 16, NBIN:] = total_im
 
     copies = []
     produce(0)
@@ -596,7 +596,7 @@
         values = jnp.dot(merged[step % 2], basis[...], preferred_element_type=jnp.float32)
         if step + 1 < steps:
             produce(step + 1)
-        lagged[step] = values.astype(jnp.bfloat16)
+        lagged[step] = (values * (1.0 / NSEG)).astype(jnp.bfloat16)
         size = per_step * rows
         copy = pltpu.make_async_copy(
             lagged.at[step], out_ref.at[pl.ds(step * size, size)], sems.at[step]
@@ -609,7 +609,7 @@
 
 def correlate(sources, receivers, basis):
     tiles = sources.shape[0]
-    rows = receivers.shape[0] * 8
+    rows = receivers.shape[0] * 16
     steps = tiles * 2
     vmem = pl.BlockSpec(memory_space=pltpu.VMEM)
     return pl.pallas_call(

time: 39.9 us -> 38.7 us (0.970)
  Pallas kernels: 39.7 us -> 38.5 us
    pallas_call x1, Pallas kernels: 4.54 us -> 3.37 us  [correlate(): pl.pallas_call(correlate_kernel, in_specs=[vmem, vmem, vmem], out_specs=p...]
where the time goes in v5:
time: 38.7 us; the launch traced here: 38.5 us
  Pallas kernels  38.5 us (99%)
    pallas_call x1, Pallas kernels, front(): pl.pallas_call(functools.partial(front_kernel, chan_count, group_count),...  35.1 us
    pallas_call x1, Pallas kernels, correlate(): pl.pallas_call(correlate_kernel, in_specs=[vmem, vmem, vmem], out_specs=p...  3.37 us

profile of v5, /device:TPU:1, one launch (start us, length us, event | category | flops | bytes accessed | tf_op | source)
XLA Modules:
  0.0 38.5 jit_solution(10121434184828610750)
XLA Ops:
  0.0 35.1 %front.1 = (bf16[4,3,16,768]{3,2,1,0:T(8,128)(2,1)S(1)}, f32[4,3,8,768]{3,2,1,0:T(8,128)S(1)}, bf16[768,512]{1,0:T(8,128)(2,1)S(1)}) custom-call(bf16[512,1024]{1,0:T(8,128)(2,1)} %strain_hbm.1, bf16[16,128]{1,0:T(8,128)(2,1)} %constant.24.back_hbm, bf16[1024,256]{1,0:T(8,128)(2,1)} %constant.25.band_hbm, s32[1,256]{1,0:T(1,128)} %bitcast.2, ...), custom_call_target="tpu_custom_call" | custom-call | tf_op jit(solution)/shard_map/front/pallas_call | solution.py:524
  35.1 3.4 %correlate.1 = bf16[2048,512]{1,0:T(8,128)(2,1)} custom-call(f32[4,3,8,768]{3,2,1,0:T(8,128)S(1)} %get-tuple-element.8.src_ref, bf16[4,3,16,768]{3,2,1,0:T(8,128)(2,1)S(1)} %get-tuple-element.9.recv_ref, bf16[768,512]{1,0:T(8,128)(2,1)S(1)} %get-tuple-element.10.basis), custom_call_target="tpu_custom_call" | custom-call | tf_op jit(solution)/shard_map/correlate/pallas_call | solution.py:615

commit v6 on v5

--- a/solution.py
+++ b/solution.py
@@ -92,7 +92,7 @@
     return jnp.concatenate(half, axis=1)
 
 
-def spectra_of(series, seg_ref, high_ref, low_ref, cos_ref, sin_ref, mask_ref, result):
+def spectra_of(series, seg_ref, table_ref, cos_ref, sin_ref, mask_ref, result):
     count = series.shape[0] - 1
     lane = lax.broadcasted_iota(jnp.int32, (8, WIDTH), 1)
     firsts = []
@@ -106,8 +106,8 @@
         edges.append(jnp.where(lane >= offset, opening, closing))
         firsts.append(first)
     flat = jnp.concatenate([local_series(series[0:count])] + edges, axis=0).astype(jnp.bfloat16)
-    part = jnp.dot(flat, high_ref[...], preferred_element_type=jnp.float32)
-    part = part + jnp.dot(flat, low_ref[...], preferred_element_type=jnp.float32)
+    twice = jnp.concatenate([flat, flat], axis=1)
+    part = jnp.dot(twice, table_ref[...], preferred_element_type=jnp.float32)
 
     def turned(base, block):
         part_re = part[base : base + 8, :NBIN]
@@ -163,8 +163,7 @@
     band_hbm,
     src_hbm,
     place_hbm,
-    high_hbm,
-    low_hbm,
+    table_hbm,
     cos_hbm,
     sin_hbm,
     mask_hbm,
@@ -178,8 +177,7 @@
     band,
     src_ref,
     place,
-    high,
-    low,
+    table,
     cos_ref,
     sin_ref,
     mask,
@@ -218,8 +216,7 @@
                 (band_hbm, band),
                 (src_hbm, src_ref),
                 (place_hbm, place),
-                (high_hbm, high),
-                (low_hbm, low),
+                (table_hbm, table),
                 (cos_hbm, cos_ref),
                 (sin_hbm, sin_ref),
                 (mask_hbm, mask),
@@ -397,11 +394,11 @@
             {"chan": me},
             MESH,
         ).wait()
-    tables = (high, low, cos_ref, sin_ref, mask, result)
+    tables = (table, cos_ref, sin_ref, mask, result)
     white[...] = spectra_of(series, seg_ref, *tables)
 
     turn = 1 - 2 * lax.rem(me, 2)
-    for step in (3, 5, 2, 6, 1, 7):
+    for step in (1, 7, 2, 6, 3, 5):
         distance = step if step < 4 else step - 8
         peer = lax.rem(plane + step, group_count)
         number = jnp.where(turn * 3 == distance, 8, 6) if step in (3, 5) else 6
@@ -500,7 +497,7 @@
     count = src_chan.shape[0]
     share = count // group_count
     back, place = halo_tables()
-    high, low = inner_tables(WIDTH)
+    table = jnp.concatenate(inner_tables(WIDTH), axis=0)
     phase_cos, phase_sin = outer_tables(WIDTH, PERIOD)
     vmem = pl.BlockSpec(memory_space=pltpu.VMEM)
     half = jnp.bfloat16
@@ -511,8 +508,7 @@
         band_table(strain.shape[1], WIDTH, 0),
         src_chan.reshape(1, count),
         place,
-        high,
-        low,
+        table,
         phase_cos,
         phase_sin,
         smooth_mask(),

time: 38.7 us -> 39.9 us (1.031)
  Pallas kernels: 38.5 us -> 39.7 us
    pallas_call x1, Pallas kernels: 35.1 us -> 36.3 us  [front(): pl.pallas_call(functools.partial(front_kernel, chan_count, group_count),...]
where the time goes in v6:
time: 39.9 us; the launch traced here: 39.7 us
  Pallas kernels  39.7 us (99%)
    pallas_call x1, Pallas kernels, front(): pl.pallas_call(functools.partial(front_kernel, chan_count, group_count),...  36.3 us
    pallas_call x1, Pallas kernels, correlate(): pl.pallas_call(correlate_kernel, in_specs=[vmem, vmem, vmem], out_specs=p...  3.37 us

profile of v6, /device:TPU:1, one launch (start us, length us, event | category | flops | bytes accessed | tf_op | source)
XLA Modules:
  0.0 39.7 jit_solution(1238676544840242493)
XLA Ops:
  0.0 36.3 %front.1 = (bf16[4,3,16,768]{3,2,1,0:T(8,128)(2,1)S(1)}, f32[4,3,8,768]{3,2,1,0:T(8,128)S(1)}, bf16[768,512]{1,0:T(8,128)(2,1)S(1)}) custom-call(bf16[512,1024]{1,0:T(8,128)(2,1)} %strain_hbm.1, bf16[16,128]{1,0:T(8,128)(2,1)} %constant.24.back_hbm, bf16[1024,256]{1,0:T(8,128)(2,1)} %constant.25.band_hbm, s32[1,256]{1,0:T(1,128)} %bitcast.2, ...), custom_call_target="tpu_custom_call" | custom-call | tf_op jit(solution)/shard_map/front/pallas_call | solution.py:520
  36.3 3.4 %correlate.1 = bf16[2048,512]{1,0:T(8,128)(2,1)} custom-call(f32[4,3,8,768]{3,2,1,0:T(8,128)S(1)} %get-tuple-element.8.src_ref, bf16[4,3,16,768]{3,2,1,0:T(8,128)(2,1)S(1)} %get-tuple-element.9.recv_ref, bf16[768,512]{1,0:T(8,128)(2,1)S(1)} %get-tuple-element.10.basis), custom_call_target="tpu_custom_call" | custom-call | tf_op jit(solution)/shard_map/correlate/pallas_call | solution.py:611

commit v7 on v6

--- a/solution.py
+++ b/solution.py
@@ -398,7 +398,7 @@
     white[...] = spectra_of(series, seg_ref, *tables)
 
     turn = 1 - 2 * lax.rem(me, 2)
-    for step in (1, 7, 2, 6, 3, 5):
+    for step in (3, 5, 2, 6, 1, 7):
         distance = step if step < 4 else step - 8
         peer = lax.rem(plane + step, group_count)
         number = jnp.where(turn * 3 == distance, 8, 6) if step in (3, 5) else 6

time: 39.9 us -> 38.7 us (0.970)
  Pallas kernels: 39.7 us -> 38.5 us
    pallas_call x1, Pallas kernels: 36.3 us -> 35.1 us  [front(): pl.pallas_call(functools.partial(front_kernel, chan_count, group_count),...]
where the time goes in v7:
time: 38.7 us; the launch traced here: 38.5 us
  Pallas kernels  38.5 us (99%)
    pallas_call x1, Pallas kernels, front(): pl.pallas_call(functools.partial(front_kernel, chan_count, group_count),...  35.1 us
    pallas_call x1, Pallas kernels, correlate(): pl.pallas_call(correlate_kernel, in_specs=[vmem, vmem, vmem], out_specs=p...  3.38 us

profile of v7, /device:TPU:1, one launch (start us, length us, event | category | flops | bytes accessed | tf_op | source)
XLA Modules:
  0.0 38.5 jit_solution(13682712342728106117)
XLA Ops:
  0.0 35.1 %front.1 = (bf16[4,3,16,768]{3,2,1,0:T(8,128)(2,1)S(1)}, f32[4,3,8,768]{3,2,1,0:T(8,128)S(1)}, bf16[768,512]{1,0:T(8,128)(2,1)S(1)}) custom-call(bf16[512,1024]{1,0:T(8,128)(2,1)} %strain_hbm.1, bf16[16,128]{1,0:T(8,128)(2,1)} %constant.24.back_hbm, bf16[1024,256]{1,0:T(8,128)(2,1)} %constant.25.band_hbm, s32[1,256]{1,0:T(1,128)} %bitcast.2, ...), custom_call_target="tpu_custom_call" | custom-call | tf_op jit(solution)/shard_map/front/pallas_call | solution.py:520
  35.1 3.4 %correlate.1 = bf16[2048,512]{1,0:T(8,128)(2,1)} custom-call(f32[4,3,8,768]{3,2,1,0:T(8,128)S(1)} %get-tuple-element.8.src_ref, bf16[4,3,16,768]{3,2,1,0:T(8,128)(2,1)S(1)} %get-tuple-element.9.recv_ref, bf16[768,512]{1,0:T(8,128)(2,1)S(1)} %get-tuple-element.10.basis), custom_call_target="tpu_custom_call" | custom-call | tf_op jit(solution)/shard_map/correlate/pallas_call | solution.py:611
